TPU v7x, 512 devices: a whole 4x4x16 slice. The times are simulated.
512 devices in a mesh: img: 32 (over z, core), row: 16 (over y, x).
Axes of the slice: x: 4, y: 4, z: 16, core: 2. Of those that a mesh axis runs over, the one named last changes fastest.
Arguments:
- features: float32 [128, 1024, 256], P('img', 'row'), may hold values from -8 to 8
- partners: int32 [128, 2], replicated, may hold values from 0 to 127, as said below
- counts: int32 [128], replicated, may hold values from 256 to 1024, as said below
- shared_proj: bfloat16 [256, 256], replicated, may hold values from -0.375 to 0.375
- value_proj: bfloat16 [256, 256], replicated, may hold values from -0.375 to 0.375
- out_proj: bfloat16 [256, 256], replicated, may hold values from -0.375 to 0.375
- ffn_in: bfloat16 [512, 512], replicated, may hold values from -0.25 to 0.25
- ffn_in_bias: float32 [512], replicated, may hold values from -3 to 3
- norm_gain: float32 [512], replicated, may hold values from 0.1 to 1.9
- norm_bias: float32 [512], replicated, may hold values from -3 to 3
- ffn_out: bfloat16 [512, 256], replicated, may hold values from -0.25 to 0.25
- ffn_out_bias: float32 [256], replicated, may hold values from -3 to 3
Outputs:
- refined: float32 [128, 1024, 256], P('img', 'row')
Inputs may be any that keep to these rules, and one draw needn't show every extreme that they name: Images form blocks of 4 consecutive ones around a cycle of blocks. Both partners of an image lie in a block at distance 1 or 2 from its own block in either direction around the cycle. Of the 8 partner entries of one block, at most 3 lie in any one of those four blocks, and in every block exactly 3 lie in one of them. Keypoint slots at positions counts[i] and beyond of image i are padding; counts may equal 1024.
All inputs are finite; a program needn't handle non-finite values.
Results may differ from a plain program's by a relative error of at most 0.004.
Values may be sent and summed in bfloat16 or wider, within the bound.
A program may use at most 64 MiB of HBM per device.

v0:
```python
import jax
import jax.numpy as jnp
from jax import lax
from jax.sharding import PartitionSpec as P

HEADS = 4
CAP = 3


OFFSETS = (1, -1, 2, -2)
NEGATIVE = -1e30


def shifted(value, axis, steps):
    count = lax.axis_size(axis)
    pairs = [(source, (source + steps) % count) for source in range(count)]
    return lax.ppermute(value, axis, pairs)


def sent_together(arrays, axis, split_dim, concat_dim, along):
    ends, at = ([], 0)
    for a in arrays[:-1]:
        at += a.shape[along]
        ends.append(at)
    both = jnp.concatenate(arrays, axis=along)
    return tuple(
        jnp.split(
            lax.all_to_all(both, axis, split_axis=split_dim, concat_axis=concat_dim, tiled=True),
            ends,
            axis=along,
        )
    )


def edge_tables(partners, my_block, img_count, per_dev):
    entries = lax.dynamic_slice_in_dim(partners, my_block * per_dev, per_dev, 0).reshape(-1)
    offset = (entries // per_dev - my_block) % img_count
    wanted = jnp.array([stride % img_count for stride in OFFSETS], jnp.int32)
    matches = offset[None, :] == wanted[:, None]
    entry_count = entries.shape[0]
    before = jnp.arange(entry_count)[:, None] > jnp.arange(entry_count)[None, :]
    earlier = jnp.sum((matches[:, None, :] & before[None, :, :]).astype(jnp.int32), axis=2)
    ranking = jnp.sum(jnp.where(matches, earlier, 0), axis=0)
    offset_kind = jnp.sum(jnp.where(matches, jnp.arange(4, dtype=jnp.int32)[:, None], 0), axis=0)
    return (entries, matches, ranking, offset_kind)


def slot_table(partners, requester, img_count, per_dev, kind_idx):
    entries, matches, ranking, _ = edge_tables(partners, requester, img_count, per_dev)
    occupied = matches[kind_idx][None, :] & (
        ranking[None, :] == jnp.arange(CAP, dtype=jnp.int32)[:, None]
    )
    filled = jnp.any(occupied, axis=1)
    image_idx = jnp.sum(jnp.where(occupied, entries % per_dev, 0), axis=1)
    edge_idx = jnp.sum(
        jnp.where(occupied, jnp.arange(entries.shape[0], dtype=jnp.int32)[None, :], 0), axis=1
    )
    return (filled, image_idx, edge_idx)


def local_softmax(scores, allowed, axis_num):
    peak_value = jnp.max(jnp.where(allowed, scores, NEGATIVE), axis=axis_num, keepdims=True)
    raised = jnp.where(allowed, jnp.exp(scores - peak_value), 0.0)
    return (raised / jnp.sum(raised, axis=axis_num, keepdims=True)).astype(jnp.bfloat16)


def per_device(
    features,
    partners,
    counts,
    shared_proj,
    value_proj,
    out_proj,
    ffn_in,
    ffn_in_bias,
    norm_gain,
    norm_bias,
    ffn_out,
    ffn_out_bias,
):
    img_count = lax.axis_size("img")
    row_devices = lax.axis_size("row")
    my_block = lax.axis_index("img")
    row_index = lax.axis_index("row")
    per_dev, row_count, feature_count = features.shape
    head_dim = feature_count // HEADS
    scale_factor = head_dim ** (-0.5)
    keypoints = row_count * row_devices
    edge_count = 2 * per_dev
    rounded = features.astype(jnp.bfloat16)
    flat_rows = rounded.reshape(per_dev * row_count, feature_count)
    shared = jnp.dot(flat_rows, shared_proj, preferred_element_type=jnp.float32).astype(
        jnp.bfloat16
    )
    values = jnp.dot(flat_rows, value_proj, preferred_element_type=jnp.float32).astype(jnp.bfloat16)
    packed = jnp.concatenate([shared, values], axis=1).reshape(
        per_dev, row_count, 2 * feature_count
    )
    entries, matches, ranking, offset_kind = edge_tables(partners, my_block, img_count, per_dev)
    position = offset_kind * CAP + ranking
    own_counts = lax.dynamic_slice_in_dim(counts, my_block * per_dev, per_dev, 0)
    partner_kp = counts[entries]
    own_slot = jnp.arange(edge_count, dtype=jnp.int32) // 2
    sender_tables = []
    asker_tables = []
    received = []
    for kind_idx, stride in enumerate(OFFSETS):
        filled, image_idx, _ = slot_table(
            partners, (my_block - stride) % img_count, img_count, per_dev, kind_idx
        )
        sender_tables.append((filled, image_idx))
        asker_tables.append(slot_table(partners, my_block, img_count, per_dev, kind_idx))
        outgoing = jnp.where(filled[:, None, None], packed[image_idx], jnp.zeros((), jnp.bfloat16))
        received.append(shifted(outgoing, "img", -stride))
    partner_rows = jnp.stack(received).reshape(4 * CAP, row_count, 2 * feature_count)[position]
    all_positions = jnp.arange(keypoints, dtype=jnp.int32)

    def by_head(source):
        edges_here = source.shape[0]
        divided = source.reshape(edges_here, row_count, 2, HEADS, head_dim)
        return divided.transpose(0, 3, 1, 2, 4).reshape(edges_here * HEADS, row_count, 2 * head_dim)

    partner_heads = by_head(partner_rows)
    own_heads = by_head(packed[own_slot])
    whole_partner, whole_own = sent_together((partner_heads, own_heads), "row", 0, 1, 2)
    item_count = whole_partner.shape[0]
    first_item = row_index * item_count
    partner_limit = lax.dynamic_slice_in_dim(
        jnp.repeat(partner_kp, HEADS), first_item, item_count, 0
    )
    own_limit = lax.dynamic_slice_in_dim(
        jnp.repeat(own_counts[own_slot], HEADS), first_item, item_count, 0
    )

    def one_item(running, scan_item):
        own_source, partner_source, own_count, partner_count = scan_item
        scores = (
            lax.dot_general(
                own_source[:, :head_dim],
                partner_source[:, :head_dim],
                (((1,), (1,)), ((), ())),
                preferred_element_type=jnp.float32,
            )
            * scale_factor
        )
        row_weights = local_softmax(scores, (all_positions < partner_count)[None, :], 1)
        column_weights = local_softmax(scores, (all_positions < own_count)[:, None], 0)
        to_own = jnp.dot(
            row_weights, partner_source[:, head_dim:], preferred_element_type=jnp.float32
        )
        to_partner = lax.dot_general(
            column_weights,
            own_source[:, head_dim:],
            (((0,), (0,)), ((), ())),
            preferred_element_type=jnp.float32,
        )
        return (running, (to_own, to_partner))

    _, (own_pieces, partner_pieces) = lax.scan(
        one_item, jnp.zeros((), jnp.float32), (whole_own, whole_partner, own_limit, partner_limit)
    )
    back_own, back_partner = sent_together((own_pieces, partner_pieces), "row", 1, 0, 2)

    def by_feature(source):
        return (
            source.reshape(edge_count, HEADS, row_count, head_dim)
            .transpose(0, 2, 1, 3)
            .reshape(edge_count, row_count, feature_count)
        )

    own_inbox = by_feature(back_own).reshape(per_dev, 2, row_count, feature_count).sum(axis=1)
    col_msgs = by_feature(back_partner)
    inbox = own_inbox
    image_range = jnp.arange(per_dev, dtype=jnp.int32)
    for kind_idx, stride in enumerate(OFFSETS):
        asked_filled, _, asked_edge = asker_tables[kind_idx]
        back = jnp.where(asked_filled[:, None, None], col_msgs[asked_edge], 0.0)
        incoming = shifted(back, "img", stride)
        sent_filled, sent_image = sender_tables[kind_idx]
        selector = (sent_filled[:, None] & (sent_image[:, None] == image_range[None, :])).astype(
            jnp.float32
        )
        inbox = inbox + jnp.einsum(
            "cl,crw->lrw", selector, incoming, precision=lax.Precision.HIGHEST
        )
    own_ids = my_block * per_dev + image_range
    degree = jnp.sum((partners.reshape(1, -1) == own_ids[:, None]).astype(jnp.float32), axis=1)
    averaged = (inbox / (2.0 + degree)[:, None, None]).astype(jnp.bfloat16)
    projected = jnp.dot(
        averaged.reshape(per_dev * row_count, feature_count),
        out_proj,
        preferred_element_type=jnp.float32,
    ).astype(jnp.bfloat16)
    joined = jnp.concatenate([flat_rows, projected], axis=1)
    hidden = jnp.dot(joined, ffn_in, preferred_element_type=jnp.float32) + ffn_in_bias
    center = jnp.mean(hidden, axis=1, keepdims=True)
    spread = jnp.mean((hidden - center) ** 2, axis=1, keepdims=True)
    normed = (hidden - center) * lax.rsqrt(spread + 1e-05) * norm_gain + norm_bias
    activated = jax.nn.gelu(normed, approximate=False).astype(jnp.bfloat16)
    update = jnp.dot(activated, ffn_out, preferred_element_type=jnp.float32) + ffn_out_bias
    return features + update.reshape(per_dev, row_count, feature_count)


def solution(mesh):
    return jax.shard_map(
        per_device,
        mesh=mesh,
        in_specs=(P("img", "row", None), P(), P(), P(), P(), P(), P(), P(), P(), P(), P(), P()),
        out_specs=P("img", "row", None),
        check_vma=False,
    )
```

profile of v0, /device:TPU:1, one launch (start us, length us, event | category | flops | bytes accessed | tf_op | source)
XLA Modules:
  0.0 134.7 jit_solution(3076834360161431051)
XLA Ops:
  0.0 0.9 constant_dynamic-slice_fusion.3
  1.1 1.0 convert_element_type.58
  2.0 1.1 convolution_convert_fusion.1
  3.2 1.1 convolution_convert_fusion.2
  6.6 0.7 select_reduce_fusion.7
  8.2 0.8 broadcast_select_fusion
  9.0 4.4 %collective-permute-start.3 = (bf16[3,64,512]{2,1,0:T(8,128)(2,1)}, bf16[3,64,512]{2,1,0:T(8,128)(2,1)S(1)}, u32[]{:S(2)}, u32[]{:S(2)}) collective-permute-start(bf16[3,64,512]{2,1,0:T(8,128)(2,1)} %broadcast_select_fusion), channel_id=1, source_target_pairs={{0,32},{16,48},{32,64},{48,80},{64,96},{80,112},{96,128},{112,144}... | collective-permute-start | bytes 589832 | tf_op jit(solution)/shard_map/ppermute | solution.py:17
  14.0 0.8 broadcast_select_fusion.1
  14.8 9.5 %collective-permute-start.2 = (bf16[3,64,512]{2,1,0:T(8,128)(2,1)}, bf16[3,64,512]{2,1,0:T(8,128)(2,1)}, u32[]{:S(2)}, u32[]{:S(2)}) collective-permute-start(bf16[3,64,512]{2,1,0:T(8,128)(2,1)} %broadcast_select_fusion.1), channel_id=1, source_target_pairs={{0,480},{16,496},{32,0},{48,16},{64,32},{80,48},{96,64},{112,80},{... | collective-permute-start | bytes 589832 | tf_op jit(solution)/shard_map/ppermute | solution.py:17
  25.2 0.8 broadcast_select_fusion.2
  26.7 0.8 broadcast_select_fusion.3
  27.4 1.0 collective-permute-start
  29.7 1.0 copy.151
  31.2 1.9 %collective-permute-done = bf16[3,64,512]{2,1,0:T(8,128)(2,1)} collective-permute-done((bf16[3,64,512]{2,1,0:T(8,128)(2,1)}, bf16[3,64,512]{2,1,0:T(8,128)(2,1)}, u32[]{:S(2)}, u32[]{:S(2)}) %collective-permute-start) | collective-permute-done | bytes 196640 | tf_op jit(solution)/shard_map/ppermute | solution.py:17
  33.1 1.2 pad_maximum_fusion.2
  35.5 1.0 copy.152
  37.0 1.1 pad_maximum_fusion
  38.2 6.8 %all-to-all-start = ((bf16[32,64,256]{2,1,0:T(8,128)(2,1)}), bf16[32,64,256]{2,1,0:T(8,128)(2,1)S(1)}, u32[]{:S(2)}, u32[]{:S(2)}) async-start(bf16[32,64,256]{2,1,0:T(8,128)(2,1)} %pad_maximum_fusion), calls=%async_computation | async-start | bytes 2097152 | tf_op jit(solution)/shard_map/all_to_all | solution.py:28
  45.1 0.7 copy.139
  48.0 12.1 %all-to-all-done = bf16[32,64,256]{2,1,0:T(8,128)(2,1)S(1)} async-done(((bf16[32,64,256]{2,1,0:T(8,128)(2,1)}), bf16[32,64,256]{2,1,0:T(8,128)(2,1)S(1)}, u32[]{:S(2)}, u32[]{:S(2)}) %all-to-all-start) | async-done | bytes 1048608 | tf_op jit(solution)/shard_map/all_to_all | solution.py:28
  60.3 17.2 %while.14 = (s32[]{:T(128)}, f32[2,1024,64]{1,2,0:T(8,128)S(1)}, f32[2,1024,64]{1,2,0:T(8,128)S(1)}, s32[2]{0:T(128)S(1)}, bf16[2,1024,128]{2,1,0:T(8,128)(2,1)S...) while((s32[]{:T(128)}, f32[2,1024,64]{1,2,0:T(8,128)S(1)}, ...), condition=%wide.region_24.25_spmd.clone.clone, body=%wide.region_19.24_spmd.clone.clone.sunk | while | flops 425719808 | bytes 19447944 | solution.py:159
  61.5 1.3 iota_compare_fusion.13
  62.9 1.1 select_reduce_fusion.17
  64.0 2.4 %fusion.180 = (f32[1024]{0:T(1024)S(1)}, f32[1024]{0:T(1024)S(1)}) fusion(f32[1024,1024]{1,0:T(8,128)S(1)} %get-tuple-element.225, f32[1024]{0:T(1024)S(1)} %get-tuple-element.226, pred[1024]{0:T(1024)(128)(4,1)S(1)} %get-tuple-element.221, f32[1024]{0:T(1024)S(1)} %get-tuple-element.227, pred[1024]{0:T(1024)(128)(4,1)S(1)} %get-tuple-element.222), kind=kLoop, calls=%fused_computation.20.clone.1 | loop fusion | flops 7337984 | bytes 4212736 | tf_op jit(solution)/shard_map/while/body/eval_jaxpr/reduce_sum | solution.py:64
  66.4 1.4 %fusion.181 = f32[2,1024,64]{1,2,0:T(8,128)S(1)} fusion(f32[2,1024,64]{1,2,0:T(8,128)S(1)} %get-tuple-element.239, s32[]{:T(128)S(6)} %copy.158, f32[1024,1024]{1,0:T(8,128)S(1)} %get-tuple-element.225, f32[1024]{0:T(1024)S(1)} %get-tuple-element.228, f32[1024]{0:T(1024)S(1)} %get-tuple-element.227, pred[1024]{0:T(1024)(128)(4,1)S(1)} %get-tuple-element.222, ...), kind=kOutput, calls=%fused_computation.26.clone.1 | convolution fusion | flops 139460608 | bytes 4727812 | tf_op jit(solution)/shard_map/while/body/eval_jaxpr/dot_general | solution.py:148
  67.8 1.2 fusion.182
  70.1 1.3 iota_compare_fusion.13
  71.5 1.1 select_reduce_fusion.17
  72.6 2.4 %fusion.180 = (f32[1024]{0:T(1024)S(1)}, f32[1024]{0:T(1024)S(1)}) fusion(f32[1024,1024]{1,0:T(8,128)S(1)} %get-tuple-element.225, f32[1024]{0:T(1024)S(1)} %get-tuple-element.226, pred[1024]{0:T(1024)(128)(4,1)S(1)} %get-tuple-element.221, f32[1024]{0:T(1024)S(1)} %get-tuple-element.227, pred[1024]{0:T(1024)(128)(4,1)S(1)} %get-tuple-element.222), kind=kLoop, calls=%fused_computation.20.clone.1 | loop fusion | flops 7337984 | bytes 4212736 | tf_op jit(solution)/shard_map/while/body/eval_jaxpr/reduce_sum | solution.py:64
  75.0 1.4 %fusion.181 = f32[2,1024,64]{1,2,0:T(8,128)S(1)} fusion(f32[2,1024,64]{1,2,0:T(8,128)S(1)} %get-tuple-element.239, s32[]{:T(128)S(6)} %copy.158, f32[1024,1024]{1,0:T(8,128)S(1)} %get-tuple-element.225, f32[1024]{0:T(1024)S(1)} %get-tuple-element.228, f32[1024]{0:T(1024)S(1)} %get-tuple-element.227, pred[1024]{0:T(1024)(128)(4,1)S(1)} %get-tuple-element.222, ...), kind=kOutput, calls=%fused_computation.26.clone.1 | convolution fusion | flops 139460608 | bytes 4727812 | tf_op jit(solution)/shard_map/while/body/eval_jaxpr/dot_general | solution.py:148
  76.4 1.2 fusion.182
  78.7 2.1 %pad_maximum_fusion.1 = f32[2,1024,128]{2,0,1:T(2,128)} fusion(f32[2,1024,64]{2,0,1:T(2,128)S(1)} %copy.127, f32[2,1024,64]{2,0,1:T(2,128)S(1)} %copy.126), kind=kLoop, calls=%fused_computation.52 | loop fusion | flops 262144 | bytes 2097152 | tf_op jit(solution)/shard_map/concatenate | solution.py:25
  80.8 4.9 %all-to-all-start.1 = ((f32[2,1024,128]{2,0,1:T(2,128)}), f32[2,1024,128]{2,0,1:T(2,128)S(1)}, u32[]{:S(2)}, u32[]{:S(2)}) async-start(f32[2,1024,128]{2,0,1:T(2,128)} %pad_maximum_fusion.1), calls=%async_computation.1 | async-start | bytes 2097152 | tf_op jit(solution)/shard_map/all_to_all | solution.py:28
  86.7 14.3 %all-to-all-done.1 = f32[2,1024,128]{2,0,1:T(2,128)S(1)} async-done(((f32[2,1024,128]{2,0,1:T(2,128)}), f32[2,1024,128]{2,0,1:T(2,128)S(1)}, u32[]{:S(2)}, u32[]{:S(2)}) %all-to-all-start.1) | async-done | bytes 1048608 | tf_op jit(solution)/shard_map/all_to_all | solution.py:28
  103.3 0.9 copy_select_fusion
  104.2 11.2 %collective-permute-start.7 = (f32[3,64,256]{2,0,1:T(4,128)}, f32[3,64,256]{2,0,1:T(4,128)S(1)}, u32[]{:S(2)}, u32[]{:S(2)}) collective-permute-start(f32[3,64,256]{2,0,1:T(4,128)} %copy_select_fusion), channel_id=1, source_target_pairs={{0,480},{16,496},{32,0},{48,16},{64,32},{80,48},{96,64},{112,80},{... | collective-permute-start | bytes 589832 | tf_op jit(solution)/shard_map/ppermute | solution.py:17
  116.0 0.9 copy_select_fusion.1
  116.8 2.1 %collective-permute-start.6 = (f32[3,64,256]{2,0,1:T(4,128)}, f32[3,64,256]{2,0,1:T(4,128)}, u32[]{:S(2)}, u32[]{:S(2)}) collective-permute-start(f32[3,64,256]{2,0,1:T(4,128)} %copy_select_fusion.1), channel_id=1, source_target_pairs={{0,32},{16,48},{32,64},{48,80},{64,96},{80,112},{96,128},{112,144}... | collective-permute-start | bytes 589832 | tf_op jit(solution)/shard_map/ppermute | solution.py:17
  119.5 0.9 copy_select_fusion.2
  120.4 0.8 collective-permute-start.5
  121.9 1.0 collective-permute-start.4
  124.3 1.0 fusion.93
  125.3 2.0 %collective-permute-done.6 = f32[3,64,256]{2,0,1:T(4,128)} collective-permute-done((f32[3,64,256]{2,0,1:T(4,128)}, f32[3,64,256]{2,0,1:T(4,128)}, u32[]{:S(2)}, u32[]{:S(2)}) %collective-permute-start.6) | collective-permute-done | bytes 196640 | tf_op jit(solution)/shard_map/ppermute | solution.py:17
  127.3 1.3 fusion.89
  128.7 1.3 fusion.85
  130.0 1.5 %fusion.23 = bf16[4,64,256]{2,0,1:T(4,128)(2,1)S(1)} fusion(f32[4,64,256]{2,0,1:T(4,128)S(1)} %fusion.93, f32[4,64,256]{2,0,1:T(4,128)S(1)} %fusion.89, f32[4,64,256]{2,0,1:T(4,128)S(1)} %fusion.85, f32[3,64,256]{2,0,1:T(4,128)} %collective-permute-done.4, f32[4,64,256]{2,1,0:T(8,128)S(1)} %reduce_sum.332, f32[4]{0:T(128)} %broadcast_add_fusion, ...), kind=kOutput, calls=%fused_computation.47 | convolution fusion | flops 2752536 | bytes 1376287 | tf_op jit(solution)/shard_map/cl,crw->lrw/dot_general | solution.py:183
  132.5 1.4 %convolution_add_fusion.1 = f32[256,256]{1,0:T(8,128)S(1)} fusion(bf16[512,256]{1,0:T(8,128)(2,1)S(1)} %copy-done.10, f32[256,512]{1,0:T(8,128)S(1)} %get-tuple-element.158, f32[512]{0:T(512)S(1)} %copy-done.12, f32[512]{0:T(512)S(1)} %copy-done.13, f32[256]{0:T(256)S(1)} %add_rsqrt_fusion, f32[256]{0:T(256)S(1)} %broadcast_multiply_fusion, ...), kind=kOutput, calls=%fused_computation.41 | convolution fusion | flops 76218368 | bytes 1055744 | tf_op jit(solution)/shard_map/dot_general | solution.py:200
  133.9 0.8 add.383
  (145 shorter events, 22.2 us)
Async XLA Ops:
  0.0 131.8 %copy-start = (bf16[512,512]{1,0:T(8,128)(2,1)S(1)}, bf16[512,512]{1,0:T(8,128)(2,1)}, u32[]{:S(2)}) copy-start(bf16[512,512]{1,0:T(8,128)(2,1)} %param.29) | copy-start | bytes 1572868
  7.6 23.1 %copy-start.6 = (s32[3]{0:T(128)}, s32[3]{0:T(128)S(1)}, u32[]{:S(2)}) copy-start(s32[3]{0:T(128)S(1)} %get-tuple-element.159) | copy-start | bytes 40
  9.0 22.2 %collective-permute-start.3 = (bf16[3,64,512]{2,1,0:T(8,128)(2,1)}, bf16[3,64,512]{2,1,0:T(8,128)(2,1)S(1)}, u32[]{:S(2)}, u32[]{:S(2)}) collective-permute-start(bf16[3,64,512]{2,1,0:T(8,128)(2,1)} %broadcast_select_fusion), channel_id=1, source_target_pairs={{0,32},{16,48},{32,64},{48,80},{64,96},{80,112},{96,128},{112,144}... | collective-permute-start | bytes 589832 | tf_op jit(solution)/shard_map/ppermute | solution.py:17
  14.8 16.4 %collective-permute-start.2 = (bf16[3,64,512]{2,1,0:T(8,128)(2,1)}, bf16[3,64,512]{2,1,0:T(8,128)(2,1)}, u32[]{:S(2)}, u32[]{:S(2)}) collective-permute-start(bf16[3,64,512]{2,1,0:T(8,128)(2,1)} %broadcast_select_fusion.1), channel_id=1, source_target_pairs={{0,480},{16,496},{32,0},{48,16},{64,32},{80,48},{96,64},{112,80},{... | collective-permute-start | bytes 589832 | tf_op jit(solution)/shard_map/ppermute | solution.py:17
  24.6 3.9 %copy-start.7 = (s32[3]{0:T(128)}, s32[3]{0:T(128)S(1)}, u32[]{:S(2)}) copy-start(s32[3]{0:T(128)S(1)} %get-tuple-element.161) | copy-start | bytes 40
  24.6 6.1 %copy-start.9 = (s32[3]{0:T(128)}, s32[3]{0:T(128)S(1)}, u32[]{:S(2)}) copy-start(s32[3]{0:T(128)S(1)} %get-tuple-element.162) | copy-start | bytes 40
  26.0 5.2 %collective-permute-start.1 = (bf16[3,64,512]{2,1,0:T(8,128)(2,1)}, bf16[3,64,512]{2,1,0:T(8,128)(2,1)}, u32[]{:S(2)}, u32[]{:S(2)}) collective-permute-start(bf16[3,64,512]{2,1,0:T(8,128)(2,1)} %broadcast_select_fusion.2), channel_id=1, source_target_pairs={{0,16},{16,32},{32,48},{48,64},{64,80},{80,96},{96,112},{112,128},... | collective-permute-start | bytes 589832 | tf_op jit(solution)/shard_map/ppermute | solution.py:17
  26.1 4.6 %copy-start.8 = (pred[3]{0:T(512)(128)(4,1)}, pred[3]{0:T(512)(128)(4,1)S(1)}, u32[]{:S(2)}) copy-start(pred[3]{0:T(512)(128)(4,1)S(1)} %fusion.98) | copy-start | bytes 13
  27.4 5.7 %collective-permute-start = (bf16[3,64,512]{2,1,0:T(8,128)(2,1)}, bf16[3,64,512]{2,1,0:T(8,128)(2,1)}, u32[]{:S(2)}, u32[]{:S(2)}) collective-permute-start(bf16[3,64,512]{2,1,0:T(8,128)(2,1)} %broadcast_select_fusion.3), channel_id=1, source_target_pairs={{0,496},{16,0},{32,16},{48,32},{64,48},{80,64},{96,80},{112,96},{1... | collective-permute-start | bytes 589832 | tf_op jit(solution)/shard_map/ppermute | solution.py:17
  35.5 9.5 %copy-start.5 = (s32[128,2]{0,1:T(2,128)S(1)}, s32[128,2]{0,1:T(2,128)}, u32[]{:S(2)}) copy-start(s32[128,2]{0,1:T(2,128)} %param.24) | copy-start | bytes 3076
  35.5 10.3 %copy-start.1 = (s32[128]{0:T(128)S(1)}, s32[128]{0:T(128)}, u32[]{:S(2)}) copy-start(s32[128]{0:T(128)} %param.25) | copy-start | bytes 1540
  38.2 21.9 %all-to-all-start = ((bf16[32,64,256]{2,1,0:T(8,128)(2,1)}), bf16[32,64,256]{2,1,0:T(8,128)(2,1)S(1)}, u32[]{:S(2)}, u32[]{:S(2)}) async-start(bf16[32,64,256]{2,1,0:T(8,128)(2,1)} %pad_maximum_fusion), calls=%async_computation | async-start | bytes 2097152 | tf_op jit(solution)/shard_map/all_to_all | solution.py:28
  80.8 20.1 %all-to-all-start.1 = ((f32[2,1024,128]{2,0,1:T(2,128)}), f32[2,1024,128]{2,0,1:T(2,128)S(1)}, u32[]{:S(2)}, u32[]{:S(2)}) async-start(f32[2,1024,128]{2,0,1:T(2,128)} %pad_maximum_fusion.1), calls=%async_computation.1 | async-start | bytes 2097152 | tf_op jit(solution)/shard_map/all_to_all | solution.py:28
  104.2 20.1 %collective-permute-start.7 = (f32[3,64,256]{2,0,1:T(4,128)}, f32[3,64,256]{2,0,1:T(4,128)S(1)}, u32[]{:S(2)}, u32[]{:S(2)}) collective-permute-start(f32[3,64,256]{2,0,1:T(4,128)} %copy_select_fusion), channel_id=1, source_target_pairs={{0,480},{16,496},{32,0},{48,16},{64,32},{80,48},{96,64},{112,80},{... | collective-permute-start | bytes 589832 | tf_op jit(solution)/shard_map/ppermute | solution.py:17
  116.8 10.5 %collective-permute-start.6 = (f32[3,64,256]{2,0,1:T(4,128)}, f32[3,64,256]{2,0,1:T(4,128)}, u32[]{:S(2)}, u32[]{:S(2)}) collective-permute-start(f32[3,64,256]{2,0,1:T(4,128)} %copy_select_fusion.1), channel_id=1, source_target_pairs={{0,32},{16,48},{32,64},{48,80},{64,96},{80,112},{96,128},{112,144}... | collective-permute-start | bytes 589832 | tf_op jit(solution)/shard_map/ppermute | solution.py:17
  120.4 8.2 %collective-permute-start.5 = (f32[3,64,256]{2,0,1:T(4,128)}, f32[3,64,256]{2,0,1:T(4,128)}, u32[]{:S(2)}, u32[]{:S(2)}) collective-permute-start(f32[3,64,256]{2,0,1:T(4,128)} %copy_select_fusion.2), channel_id=1, source_target_pairs={{0,496},{16,0},{32,16},{48,32},{64,48},{80,64},{96,80},{112,96},{1... | collective-permute-start | bytes 589832 | tf_op jit(solution)/shard_map/ppermute | solution.py:17
  121.9 8.1 %collective-permute-start.4 = (f32[3,64,256]{2,0,1:T(4,128)S(1)}, f32[3,64,256]{2,0,1:T(4,128)}, u32[]{:S(2)}, u32[]{:S(2)}) collective-permute-start(f32[3,64,256]{2,0,1:T(4,128)S(1)} %copy_select_fusion.3), channel_id=1, source_target_pairs={{0,16},{16,32},{32,48},{48,64},{64,80},{80,96},{96,112},{112,128},... | collective-permute-start | bytes 589832 | tf_op jit(solution)/shard_map/ppermute | solution.py:17
  122.9 8.6 %copy-start.3 = (bf16[256,256]{1,0:T(8,128)(2,1)S(1)}, bf16[256,256]{1,0:T(8,128)(2,1)}, u32[]{:S(2)}) copy-start(bf16[256,256]{1,0:T(8,128)(2,1)} %param.28) | copy-start | bytes 393220
  123.6 8.2 %copy-start.4 = (bf16[256,256]{0,1:T(8,128)(2,1)S(1)}, bf16[256,256]{0,1:T(8,128)(2,1)}, u32[]{:S(2)}) copy-start(bf16[256,256]{0,1:T(8,128)(2,1)} %copy.139) | copy-start | bytes 393220
  123.6 8.2 %copy-start.11 = (f32[512]{0:T(512)S(1)}, f32[512]{0:T(512)}, u32[]{:S(2)}) copy-start(f32[512]{0:T(512)} %param.30) | copy-start | bytes 6148
  123.6 8.8 %copy-start.10 = (bf16[512,256]{1,0:T(8,128)(2,1)S(1)}, bf16[512,256]{1,0:T(8,128)(2,1)}, u32[]{:S(2)}) copy-start(bf16[512,256]{1,0:T(8,128)(2,1)} %param.33) | copy-start | bytes 786436
  123.6 8.8 %copy-start.12 = (f32[512]{0:T(512)S(1)}, f32[512]{0:T(512)}, u32[]{:S(2)}) copy-start(f32[512]{0:T(512)} %param.32) | copy-start | bytes 6148
  123.6 8.8 %copy-start.13 = (f32[512]{0:T(512)S(1)}, f32[512]{0:T(512)}, u32[]{:S(2)}) copy-start(f32[512]{0:T(512)} %param.31) | copy-start | bytes 6148
  123.6 8.8 %copy-start.14 = (f32[256]{0:T(256)S(1)}, f32[256]{0:T(256)}, u32[]{:S(2)}) copy-start(f32[256]{0:T(256)} %param.34) | copy-start | bytes 3076
  132.5 1.4 %copy-start.2 = (f32[4,64,256]{2,1,0:T(8,128)S(1)}, f32[4,64,256]{2,1,0:T(8,128)}, u32[]{:S(2)}) copy-start(f32[4,64,256]{2,1,0:T(8,128)} %param.23) | copy-start | bytes 786436
where the time goes:
time: 135 us
  starting transfers between devices  41.5 us (31%)
  waiting for transfers between devices  30.3 us (22%)
  other arithmetic  23.6 us (17%)
  local copies, waits for them, and re-layouts  21.6 us (16%)
  matrix products  16.8 us (12%)
    ppermute x8, starting transfers between devices, shifted(): return lax.ppermute(value, axis, pairs)  29.9 us
    all_to_all x2, waiting for transfers between devices, sent_together(): lax.all_to_all(both, axis, split_axis=split_dim, concat_axis=concat_dim,...  26.3 us
    all_to_all x2, starting transfers between devices, sent_together(): lax.all_to_all(both, axis, split_axis=split_dim, concat_axis=concat_dim,...  11.6 us
    dot_general x4, matrix products, per_device(): jnp.einsum('cl,crw->lrw', selector, incoming, precision=lax.Precision.HIG...  5.1 us
    reduce_sum x2, other arithmetic, local_softmax(): jnp.sum(raised, axis=axis_num, keepdims=True)  4.79 us
    ppermute x8, waiting for transfers between devices, shifted(): return lax.ppermute(value, axis, pairs)  3.97 us
    concatenate x2, other arithmetic, sent_together(): both = jnp.concatenate(arrays, axis=along)  3.28 us
    reshape x4, local copies, waits for them, and re-layouts, by_head(): divided = source.reshape(edges_here, row_count, 2, HEADS, head_dim)  3.1 us
  transfers between devices with their start and end apart: 10, of which 4 were waited for; matrix products, arithmetic and copies ran while one was open for 15% of the time, Pallas kernels for 0%

commit v1 on v0

v1 whole, which is shorter than its diff:
```python
import functools

import jax
import jax.numpy as jnp
from jax import lax
from jax.experimental import pallas as pl
from jax.experimental.pallas import tpu as pltpu
from jax.sharding import PartitionSpec as P

HEADS = 4
CAP = 3
OFFSETS = (1, -1, 2, -2)
PENALTY = -1e30
MESH = pl.DeviceIdType.MESH
F32 = jnp.float32
BF16 = jnp.bfloat16


def peer_order(count):
    if count == 16:
        return (1, 4, 15, 12, 5, 11, 3, 13, 2, 8, 6, 9, 14, 7, 10)
    return tuple(range(1, count))


def lanes(shape):
    return lax.broadcasted_iota(jnp.int32, shape, len(shape) - 1)


def kernel(
    img_count,
    row_devices,
    partners,
    counts,
    x_ref,
    wq_ref,
    wv_ref,
    wo_ref,
    f1_ref,
    b1_ref,
    gain_ref,
    nbias_ref,
    f2_ref,
    b2_ref,
    out_ref,
    xb,
    wh,
    w2,
    hid,
    zrecv,
    own_send,
    own_recv,
    part_send,
    part_recv,
    k_own,
    v_own,
    k_part,
    v_part,
    ret_acc,
    ret_send,
    msg_recv,
    sum_recv,
    back_send,
    back_recv,
    proj,
    z_send_sem,
    z_recv_sem,
    a_send_sem,
    a_recv_sem,
    l_sem,
    b_send_sem,
    b_recv_sem,
):
    per_dev, rows, width = x_ref.shape
    half = rows // 2
    head_dim = width // HEADS_OF(width)
    heads = width // head_dim
    pair = 2 * head_dim
    keypoints = rows * row_devices
    edges = 2 * per_dev
    scale = head_dim ** (-0.5)
    block = lax.axis_index("img")
    me = lax.axis_index("row")
    my_image = lax.div(me, heads)
    order = peer_order(row_devices)

    def img_peer(offset):
        return lax.rem(block + (offset + img_count), img_count)

    def row_peer(offset):
        return lax.rem(me + offset, row_devices)

    barrier = pltpu.get_barrier_semaphore()
    for offset in OFFSETS:
        pl.semaphore_signal(barrier, inc=1, device_id=(img_peer(offset), me), device_id_type=MESH)
    for offset in order:
        pl.semaphore_signal(
            barrier, inc=1, device_id=(block, row_peer(offset)), device_id_type=MESH
        )

    xb[...] = x_ref[...].astype(BF16)

    low = lanes((width, pair)) < head_dim
    for t in range(width // pair):
        q_t = wq_ref[:, t * pair : (t + 1) * pair].astype(F32)
        v_t = wv_ref[:, t * pair : (t + 1) * pair].astype(F32)
        first = jnp.where(low, q_t, pltpu.roll(v_t, head_dim, 1))
        second = jnp.where(low, pltpu.roll(q_t, head_dim, 1), v_t)
        wh[:, 2 * t * pair : (2 * t + 1) * pair] = first.astype(BF16)
        wh[:, (2 * t + 1) * pair : (2 * t + 2) * pair] = second.astype(BF16)

    pl.semaphore_wait(barrier, len(OFFSETS) + len(order))

    z_copies = []
    for kind, offset in enumerate(OFFSETS):
        copy = pltpu.make_async_remote_copy(
            src_ref=xb,
            dst_ref=zrecv.at[pl.ds(kind * per_dev, per_dev)],
            send_sem=z_send_sem.at[kind],
            recv_sem=z_recv_sem.at[kind],
            device_id=(img_peer(-offset), me),
            device_id_type=MESH,
        )
        copy.start()
        z_copies.append(copy)

    def spread(phase, send, recv):
        for offset in order:
            peer = row_peer(offset)
            pltpu.make_async_remote_copy(
                src_ref=send.at[peer],
                dst_ref=recv.at[me],
                send_sem=a_send_sem.at[phase],
                recv_sem=a_recv_sem.at[phase],
                device_id=(block, peer),
                device_id_type=MESH,
            ).start()
        pltpu.make_async_copy(send.at[me], recv.at[me], l_sem.at[phase]).start()

    def arrived(phase, send, recv):
        rest = pl.ds(0, row_devices - 1)
        pltpu.make_async_copy(recv.at[rest], recv.at[rest], a_recv_sem.at[phase]).wait()
        pltpu.make_async_copy(send.at[me], recv.at[me], l_sem.at[phase]).wait()

    def left(phase, send):
        rest = pl.ds(0, row_devices - 1)
        pltpu.make_async_copy(send.at[rest], send.at[rest], a_send_sem.at[phase]).wait()

    def projected_heads(source, send, image):
        both = jnp.dot(source, wh[...], preferred_element_type=F32).astype(BF16)
        for h in range(heads):
            send[image * heads + h] = both[:, h * pair : (h + 1) * pair]

    for image in range(per_dev):
        projected_heads(xb[image], own_send, image)
    spread(0, own_send, own_recv)

    def kind_of(entry, home):
        away = lax.rem(lax.div(entry, per_dev) - home + 2 * img_count, img_count)
        return jnp.where(
            away == 1, 0, jnp.where(away == img_count - 1, 1, jnp.where(away == 2, 2, 3))
        )

    my_entries = [partners[block * edges + e] for e in range(edges)]
    my_kinds = [kind_of(entry, block) for entry in my_entries]

    hid[...] = (
        jnp.dot(
            xb[...].reshape(per_dev * rows, width),
            f1_ref[0:width, :],
            preferred_element_type=F32,
        )
        + b1_ref[...]
    )
    for h in range(heads):
        piece = wo_ref[h * head_dim : (h + 1) * head_dim, :]
        blank = jnp.zeros_like(piece)
        w2[h * pair : h * pair + head_dim, 0:width] = blank
        w2[h * pair : h * pair + head_dim, width : 2 * width] = piece
        w2[h * pair + head_dim : (h + 1) * pair, 0:width] = piece
        w2[h * pair + head_dim : (h + 1) * pair, width : 2 * width] = blank

    for copy in z_copies:
        copy.wait()
    for j in range(2):
        for image in range(per_dev):
            e = 2 * image + j
            at = my_kinds[e] * per_dev + lax.rem(my_entries[e], per_dev)
            projected_heads(zrecv[at], part_send.at[j], image)
        spread(1 + j, part_send.at[j], part_recv.at[j])

    chunk = min(256, keypoints)
    lane = lanes((keypoints, pair))
    place = lax.broadcasted_iota(jnp.int32, (keypoints, pair), 0)

    def prepare(source, count, k_ref, v_ref):
        flat = source[...].reshape(keypoints, pair).astype(F32)
        penalty = jnp.where((lane == head_dim) & (place >= count), PENALTY, 0.0)
        k_ref[...] = jnp.where(lane < head_dim, flat * scale, penalty).astype(BF16).T
        v_ref[...] = jnp.where(
            lane >= head_dim, flat, jnp.where(lane == 0, 1.0, 0.0)
        ).astype(BF16)

    def attend(asking, k_ref, v_ref, finish):
        per_chunk = chunk // rows
        low_chunk = lanes((chunk, pair)) < head_dim
        low_half = lanes((chunk // 2, pair)) < head_dim

        def one_chunk(c, carry):
            q = asking[pl.ds(c * per_chunk, per_chunk)].reshape(chunk, pair)
            q = jnp.where(low_chunk, q, jnp.ones((), BF16))
            scores = jnp.dot(q, k_ref[...], preferred_element_type=F32)
            peak = jnp.max(scores, axis=1, keepdims=True)
            raised = jnp.exp(scores - peak).astype(BF16)
            total = jnp.dot(raised, v_ref[...], preferred_element_type=F32)
            message = total / total[:, 0:1]
            split = message.reshape(per_chunk, 2, half, pair)
            upper = split[:, 0].reshape(chunk // 2, pair)
            lower = pltpu.roll(split[:, 1].reshape(chunk // 2, pair), head_dim, 1)
            finish(c, per_chunk, jnp.where(low_half, lower, upper).reshape(per_chunk, half, pair))
            return carry

        lax.fori_loop(0, keypoints // chunk, one_chunk, 0)

    arrived(0, own_send, own_recv)
    prepare(own_recv, counts[block * per_dev + my_image], k_own, v_own)
    for j in range(2):
        arrived(1 + j, part_send.at[j], part_recv.at[j])
        asked = partners[block * edges + 2 * my_image + j]
        prepare(part_recv.at[j], counts[asked], k_part, v_part)

        def to_partner(c, n, message, j=j):
            ret_send[j, pl.ds(c * n, n)] = message.astype(BF16)

        def to_own(c, n, message, j=j):
            if j == 0:
                ret_acc[pl.ds(c * n, n)] = message
            else:
                ret_send[2, pl.ds(c * n, n)] = (ret_acc[pl.ds(c * n, n)] + message).astype(BF16)

        attend(part_recv.at[j], k_own, v_own, to_partner)
        spread(3 + j, ret_send.at[j], msg_recv.at[j])
        attend(own_recv, k_part, v_part, to_own)
    spread(5, ret_send.at[2], sum_recv)

    def ranks_of(kinds):
        ranks = []
        for e in range(edges):
            rank = jnp.int32(0)
            for before in range(e):
                rank = rank + jnp.where(kinds[before] == kinds[e], 1, 0)
            ranks.append(rank)
        return ranks

    my_ranks = ranks_of(my_kinds)
    arrived(3, ret_send.at[0], msg_recv.at[0])
    arrived(4, ret_send.at[1], msg_recv.at[1])
    back_copies = []
    for kind, offset in enumerate(OFFSETS):
        for c in range(CAP):
            edge = jnp.int32(0)
            for e in range(edges):
                edge = edge + jnp.where((my_kinds[e] == kind) & (my_ranks[e] == c), e, 0)
            image, j = lax.div(edge, 2), lax.rem(edge, 2)
            back_send[kind, c] = msg_recv[j, pl.ds(image * heads, heads)]
        copy = pltpu.make_async_remote_copy(
            src_ref=back_send.at[kind],
            dst_ref=back_recv.at[kind],
            send_sem=b_send_sem.at[kind],
            recv_sem=b_recv_sem.at[kind],
            device_id=(img_peer(offset), me),
            device_id_type=MESH,
        )
        copy.start()
        back_copies.append(copy)

    weights = []
    for kind, offset in enumerate(OFFSETS):
        source = img_peer(-offset)
        entries = [partners[source * edges + e] for e in range(edges)]
        kinds = [kind_of(entry, source) for entry in entries]
        ranks = ranks_of(kinds)
        for c in range(CAP):
            row = []
            for image in range(per_dev):
                hit = jnp.int32(0)
                for e in range(edges):
                    hit = hit + jnp.where(
                        (kinds[e] == kind)
                        & (ranks[e] == c)
                        & (lax.rem(entries[e], per_dev) == image),
                        1,
                        0,
                    )
                row.append(hit)
            weights.append(row)

    arrived(5, ret_send.at[2], sum_recv)
    for copy in back_copies:
        copy.wait()

    packed = []
    for image in range(per_dev):
        inbox = sum_recv[image * heads : (image + 1) * heads].astype(F32)
        degree = jnp.int32(2)
        for kind in range(len(OFFSETS)):
            for c in range(CAP):
                hit = weights[kind * CAP + c][image]
                degree = degree + hit
                inbox = inbox + hit.astype(F32) * back_recv[kind, c].astype(F32)
        packed.append((inbox / degree.astype(F32)).astype(BF16))
    stacked = jnp.concatenate(
        [jnp.concatenate([packed[i][h] for i in range(per_dev)], axis=0) for h in range(heads)],
        axis=1,
    )
    both = jnp.dot(stacked, w2[...], preferred_element_type=F32).astype(BF16)
    for image in range(per_dev):
        mine = both[image * half : (image + 1) * half]
        proj[image * rows : image * rows + half, :] = mine[:, 0:width]
        proj[image * rows + half : (image + 1) * rows, :] = mine[:, width : 2 * width]

    for image in range(per_dev):
        part = pl.ds(image * rows, rows)
        hidden = hid[part, :] + jnp.dot(
            proj[part, :], f1_ref[width : 2 * width, :], preferred_element_type=F32
        )
        center = jnp.mean(hidden, axis=1, keepdims=True)
        away = hidden - center
        spreads = jnp.mean(away * away, axis=1, keepdims=True)
        normed = away * lax.rsqrt(spreads + 1e-5) * gain_ref[...] + nbias_ref[...]
        active = (0.5 * normed * (1.0 + lax.erf(normed * (0.5**0.5)))).astype(BF16)
        out_ref[image] = (
            x_ref[image]
            + jnp.dot(active, f2_ref[...], preferred_element_type=F32)
            + b2_ref[...]
        )

    for phase, send in (
        (0, own_send),
        (1, part_send.at[0]),
        (2, part_send.at[1]),
        (3, ret_send.at[0]),
        (4, ret_send.at[1]),
        (5, ret_send.at[2]),
    ):
        left(phase, send)


def HEADS_OF(width):
    return width // 64


def per_device(
    features,
    partners,
    counts,
    shared_proj,
    value_proj,
    out_proj,
    ffn_in,
    ffn_in_bias,
    norm_gain,
    norm_bias,
    ffn_out,
    ffn_out_bias,
):
    img_count = lax.axis_size("img")
    row_devices = lax.axis_size("row")
    per_dev, rows, width = features.shape
    heads = HEADS_OF(width)
    head_dim = width // heads
    pair = 2 * head_dim
    keypoints = rows * row_devices
    hidden = ffn_in.shape[1]
    half = rows // 2
    kinds = len(OFFSETS)
    vmem = pl.BlockSpec(memory_space=pltpu.VMEM)
    smem = pl.BlockSpec(memory_space=pltpu.SMEM)
    return pl.pallas_call(
        functools.partial(kernel, img_count, row_devices),
        out_shape=jax.ShapeDtypeStruct(features.shape, F32),
        in_specs=[smem, smem] + [vmem] * 10,
        out_specs=vmem,
        scratch_shapes=[
            pltpu.VMEM((per_dev, rows, width), BF16),
            pltpu.VMEM((width, 2 * width), BF16),
            pltpu.VMEM((heads * pair, 2 * width), BF16),
            pltpu.VMEM((per_dev * rows, hidden), F32),
            pltpu.VMEM((kinds * per_dev, rows, width), BF16),
            pltpu.VMEM((row_devices, rows, pair), BF16),
            pltpu.VMEM((row_devices, rows, pair), BF16),
            pltpu.VMEM((2, row_devices, rows, pair), BF16),
            pltpu.VMEM((2, row_devices, rows, pair), BF16),
            pltpu.VMEM((pair, keypoints), BF16),
            pltpu.VMEM((keypoints, pair), BF16),
            pltpu.VMEM((pair, keypoints), BF16),
            pltpu.VMEM((keypoints, pair), BF16),
            pltpu.VMEM((row_devices, half, pair), F32),
            pltpu.VMEM((3, row_devices, half, pair), BF16),
            pltpu.VMEM((2, row_devices, half, pair), BF16),
            pltpu.VMEM((row_devices, half, pair), BF16),
            pltpu.VMEM((kinds, CAP, heads, half, pair), BF16),
            pltpu.VMEM((kinds, CAP, heads, half, pair), BF16),
            pltpu.VMEM((per_dev * rows, width), BF16),
            pltpu.SemaphoreType.DMA((kinds,)),
            pltpu.SemaphoreType.DMA((kinds,)),
            pltpu.SemaphoreType.DMA((6,)),
            pltpu.SemaphoreType.DMA((6,)),
            pltpu.SemaphoreType.DMA((6,)),
            pltpu.SemaphoreType.DMA((kinds,)),
            pltpu.SemaphoreType.DMA((kinds,)),
        ],
        compiler_params=pltpu.CompilerParams(
            collective_id=0, has_side_effects=True, vmem_limit_bytes=48 * 1024 * 1024
        ),
    )(
        partners.reshape(-1),
        counts,
        features,
        shared_proj,
        value_proj,
        out_proj,
        ffn_in,
        ffn_in_bias.reshape(1, -1),
        norm_gain.reshape(1, -1),
        norm_bias.reshape(1, -1),
        ffn_out,
        ffn_out_bias.reshape(1, -1),
    )


def solution(mesh):
    return jax.shard_map(
        per_device,
        mesh=mesh,
        in_specs=(P("img", "row", None), P(), P(), P(), P(), P(), P(), P(), P(), P(), P(), P()),
        out_specs=P("img", "row", None),
        check_vma=False,
    )
```

time: 135 us -> 54.7 us (0.41)
  Pallas kernels: 0 us -> 47.4 us
  starting transfers between devices: 41.5 us -> 0 us
  waiting for transfers between devices: 30.3 us -> 0 us
  other arithmetic: 23.6 us -> 0 us
  matrix products: 16.8 us -> 0 us
  local copies, waits for them, and re-layouts: 21.6 us -> 6.97 us
    pallas_call x0 -> x1, Pallas kernels: none -> 47.4 us  [per_device(): pl.pallas_call(functools.partial(kernel, img_count, row_devices), out_sha...]
    ppermute x8 -> x0, starting transfers between devices: 29.9 us -> none  [shifted(): return lax.ppermute(value, axis, pairs)]
    all_to_all x2 -> x0, waiting for transfers between devices: 26.3 us -> none  [sent_together(): lax.all_to_all(both, axis, split_axis=split_dim, concat_axis=concat_dim,...]
    dot_general x15 -> x0, matrix products: 16.8 us -> none  [the longest x4 5.1 us: per_device(): jnp.einsum('cl,crw->lrw', selector, incoming, precision=lax.Precision.HIG...]
    all_to_all x2 -> x0, starting transfers between devices: 11.6 us -> none  [sent_together(): lax.all_to_all(both, axis, split_axis=split_dim, concat_axis=concat_dim,...]
    reshape x18 -> x1, local copies, waits for them, and re-layouts: 7.42 us -> 0.14 us  [per_device(): partners.reshape(-1)]
    gather x12 -> x0, local copies, waits for them, and re-layouts: 6.93 us -> none  [the longest x4 2.24 us: per_device(): back = jnp.where(asked_filled[:, None, None], col_msgs[asked_edge], 0.0)]
    reduce_sum x10 -> x0, other arithmetic: 6.84 us -> none  [the longest x2 4.79 us: local_softmax(): jnp.sum(raised, axis=axis_num, keepdims=True)]
  transfers between devices with their start and end apart: 10 -> 0, of which waited for: 4 -> 0; matrix products, arithmetic and copies ran while one was open for 15% -> 0% of each run, Pallas kernels for 0% -> 0%
where the time goes in v1:
time: 54.7 us; the launch traced here: 54.4 us
  Pallas kernels  47.4 us (87%)
  local copies, waits for them, and re-layouts  6.97 us (13%)
    pallas_call x1, Pallas kernels, per_device(): pl.pallas_call(functools.partial(kernel, img_count, row_devices), out_sha...  47.4 us
    unnamed x24, local copies, waits for them, and re-layouts  6.83 us

profile of v1, /device:TPU:1, one launch (start us, length us, event | category | flops | bytes accessed | tf_op | source)
XLA Modules:
  0.0 54.4 jit_solution(11088461002146381100)
XLA Ops:
  0.0 0.0 copy-start.3
  0.0 0.8 %copy.13 = s32[128,2]{1,0:T(8,128)S(1)} copy(s32[128,2]{0,1:T(2,128)} %param.13) | data formatting | bytes 2048 | tf_op args[1]
  0.8 0.0 copy-start.6
  0.8 0.0 copy-start.7
  0.8 0.0 copy-start.8
  0.9 0.0 copy-start.9
  0.9 0.0 copy-start.10
  0.9 0.1 reshape.15.partners
  1.0 0.0 copy-done.3
  1.0 0.5 copy-done.6
  1.5 0.0 copy-done.7
  1.5 0.0 copy-done.8
  1.6 0.0 copy-done.9
  1.6 0.0 copy-done.10
  1.6 0.0 copy-start
  1.6 1.0 %copy-done = bf16[512,512]{1,0:T(8,128)(2,1)S(1)} copy-done((bf16[512,512]{1,0:T(8,128)(2,1)S(1)}, bf16[512,512]{1,0:T(8,128)(2,1)}, u32[]{:S(2)}) %copy-start) | copy-done | bytes 524312
  2.6 0.0 copy-start.1
  2.6 0.9 %copy-done.1 = f32[4,64,256]{2,1,0:T(8,128)S(1)} copy-done((f32[4,64,256]{2,1,0:T(8,128)S(1)}, f32[4,64,256]{2,1,0:T(8,128)}, u32[]{:S(2)}) %copy-start.1) | copy-done | bytes 262168
  3.6 0.0 copy-start.2
  3.6 0.9 %copy-done.2 = bf16[512,256]{1,0:T(8,128)(2,1)S(1)} copy-done((bf16[512,256]{1,0:T(8,128)(2,1)S(1)}, bf16[512,256]{1,0:T(8,128)(2,1)}, u32[]{:S(2)}) %copy-start.2) | copy-done | bytes 262168
  4.5 0.0 copy-start.4
  4.5 0.9 %copy-done.4 = bf16[256,256]{1,0:T(8,128)(2,1)S(1)} copy-done((bf16[256,256]{1,0:T(8,128)(2,1)S(1)}, bf16[256,256]{1,0:T(8,128)(2,1)}, u32[]{:S(2)}) %copy-start.4) | copy-done | bytes 131096
  5.4 0.0 copy-start.5
  5.4 0.9 %copy-done.5 = bf16[256,256]{1,0:T(8,128)(2,1)S(1)} copy-done((bf16[256,256]{1,0:T(8,128)(2,1)S(1)}, bf16[256,256]{1,0:T(8,128)(2,1)}, u32[]{:S(2)}) %copy-start.5) | copy-done | bytes 131096
  6.3 47.4 %shard_map.118 = f32[4,64,256]{2,1,0:T(8,128)S(1)} custom-call(s32[256]{0:T(256)S(1)} %reshape.15.partners, s32[128]{0:T(128)S(1)} %copy-done.10, f32[4,64,256]{2,1,0:T(8,128)S(1)} %copy-done.1, bf16[256,256]{1,0:T(8,128)(2,1)S(1)} %copy-done.3, bf16[256,256]{1,0:T(8,128)(2,1)S(1)} %copy-done.4, bf16[256,256]{1,0:T(8,128)(2,1)S(1)} %copy-done.5, ...), custom_call_target="tpu_custom_call" | custom-call | tf_op jit(solution)/shard_map/pallas_call | solution.py:378
  53.7 0.7 %copy.15 = f32[4,64,256]{2,1,0:T(8,128)} copy(f32[4,64,256]{2,1,0:T(8,128)S(1)} %shard_map.118) | data formatting | bytes 524288
Async XLA Ops:
  0.0 1.0 %copy-start.3 = (bf16[256,256]{1,0:T(8,128)(2,1)S(1)}, bf16[256,256]{1,0:T(8,128)(2,1)}, u32[]{:S(2)}) copy-start(bf16[256,256]{1,0:T(8,128)(2,1)} %wq_ref.1) | copy-start | bytes 393220
  0.8 0.7 %copy-start.6 = (f32[512]{0:T(512)S(1)}, f32[512]{0:T(512)}, u32[]{:S(2)}) copy-start(f32[512]{0:T(512)} %param.19) | copy-start | bytes 6148
  0.8 0.7 %copy-start.7 = (f32[512]{0:T(512)S(1)}, f32[512]{0:T(512)}, u32[]{:S(2)}) copy-start(f32[512]{0:T(512)} %param.20) | copy-start | bytes 6148
  0.8 0.7 %copy-start.8 = (f32[512]{0:T(512)S(1)}, f32[512]{0:T(512)}, u32[]{:S(2)}) copy-start(f32[512]{0:T(512)} %param.21) | copy-start | bytes 6148
  0.9 0.7 %copy-start.9 = (f32[256]{0:T(256)S(1)}, f32[256]{0:T(256)}, u32[]{:S(2)}) copy-start(f32[256]{0:T(256)} %param.23) | copy-start | bytes 3076
  0.9 0.7 %copy-start.10 = (s32[128]{0:T(128)S(1)}, s32[128]{0:T(128)}, u32[]{:S(2)}) copy-start(s32[128]{0:T(128)} %counts.1) | copy-start | bytes 1540
  1.6 1.0 %copy-start = (bf16[512,512]{1,0:T(8,128)(2,1)S(1)}, bf16[512,512]{1,0:T(8,128)(2,1)}, u32[]{:S(2)}) copy-start(bf16[512,512]{1,0:T(8,128)(2,1)} %f1_ref.1) | copy-start | bytes 1572868
  2.6 0.9 %copy-start.1 = (f32[4,64,256]{2,1,0:T(8,128)S(1)}, f32[4,64,256]{2,1,0:T(8,128)}, u32[]{:S(2)}) copy-start(f32[4,64,256]{2,1,0:T(8,128)} %x_ref.1) | copy-start | bytes 786436
  3.6 0.9 %copy-start.2 = (bf16[512,256]{1,0:T(8,128)(2,1)S(1)}, bf16[512,256]{1,0:T(8,128)(2,1)}, u32[]{:S(2)}) copy-start(bf16[512,256]{1,0:T(8,128)(2,1)} %f2_ref.1) | copy-start | bytes 786436
  4.5 0.9 %copy-start.4 = (bf16[256,256]{1,0:T(8,128)(2,1)S(1)}, bf16[256,256]{1,0:T(8,128)(2,1)}, u32[]{:S(2)}) copy-start(bf16[256,256]{1,0:T(8,128)(2,1)} %wv_ref.1) | copy-start | bytes 393220
  5.4 0.9 %copy-start.5 = (bf16[256,256]{1,0:T(8,128)(2,1)S(1)}, bf16[256,256]{1,0:T(8,128)(2,1)}, u32[]{:S(2)}) copy-start(bf16[256,256]{1,0:T(8,128)(2,1)} %wo_ref.1) | copy-start | bytes 393220

commit v2 on v1

--- a/solution.py
+++ b/solution.py
@@ -29,6 +29,19 @@
 def kernel(
     img_count,
     row_devices,
+    partners_hbm,
+    counts_hbm,
+    x_hbm,
+    wq_hbm,
+    wv_hbm,
+    wo_hbm,
+    f1_hbm,
+    b1_hbm,
+    gain_hbm,
+    nbias_hbm,
+    f2_hbm,
+    b2_hbm,
+    out_hbm,
     partners,
     counts,
     x_ref,
@@ -42,7 +55,10 @@
     f2_ref,
     b2_ref,
     out_ref,
+    in_sem,
+    out_sem,
     xb,
+    zsend,
     wh,
     w2,
     hid,
@@ -89,6 +105,28 @@
     def row_peer(offset):
         return lax.rem(me + offset, row_devices)
 
+    loads = [
+        pltpu.make_async_copy(source, target, in_sem.at[n])
+        for n, (source, target) in enumerate(
+            (
+                (partners_hbm, partners),
+                (counts_hbm, counts),
+                (x_hbm, x_ref),
+                (wq_hbm, wq_ref),
+                (wv_hbm, wv_ref),
+                (f1_hbm, f1_ref),
+                (b1_hbm, b1_ref),
+                (wo_hbm, wo_ref),
+                (gain_hbm, gain_ref),
+                (nbias_hbm, nbias_ref),
+                (f2_hbm, f2_ref),
+                (b2_hbm, b2_ref),
+            )
+        )
+    ]
+    for load in loads:
+        load.start()
+
     barrier = pltpu.get_barrier_semaphore()
     for offset in OFFSETS:
         pl.semaphore_signal(barrier, inc=1, device_id=(img_peer(offset), me), device_id_type=MESH)
@@ -97,8 +135,53 @@
             barrier, inc=1, device_id=(block, row_peer(offset)), device_id_type=MESH
         )
 
+    def entries_of(home):
+        return [partners[e % 2, home * per_dev + e // 2] for e in range(edges)]
+
+    def slots_between(entries, target):
+        found, count = [], jnp.int32(0)
+        for entry in entries:
+            inside = lax.div(entry, per_dev) == target
+            found.append((inside, count))
+            count = count + jnp.where(inside, 1, 0)
+        slots = []
+        for c in range(CAP):
+            edge, image = jnp.int32(0), jnp.int32(0)
+            for e, (inside, rank) in enumerate(found):
+                here = inside & (rank == c)
+                edge = jnp.where(here, e + 1, edge)
+                image = jnp.where(here, lax.rem(entries[e], per_dev) + 1, image)
+            slots.append((edge, image))
+        return found, slots
+
+    loads[0].wait()
+    incoming_slots = []
+    for kind, offset in enumerate(OFFSETS):
+        _, slots = slots_between(entries_of(img_peer(-offset)), block)
+        incoming_slots.append([image for _, image in slots])
+    loads[2].wait()
     xb[...] = x_ref[...].astype(BF16)
-
+    for kind in range(len(OFFSETS)):
+        for c in range(CAP):
+            zsend[kind, c] = xb[jnp.maximum(incoming_slots[kind][c] - 1, 0)]
+
+    pl.semaphore_wait(barrier, len(OFFSETS) + len(order))
+
+    z_copies = []
+    for kind, offset in enumerate(OFFSETS):
+        copy = pltpu.make_async_remote_copy(
+            src_ref=zsend.at[kind],
+            dst_ref=zrecv.at[pl.ds(kind * CAP, CAP)],
+            send_sem=z_send_sem.at[kind],
+            recv_sem=z_recv_sem.at[kind],
+            device_id=(img_peer(-offset), me),
+            device_id_type=MESH,
+        )
+        copy.start()
+        z_copies.append(copy)
+
+    loads[3].wait()
+    loads[4].wait()
     low = lanes((width, pair)) < head_dim
     for t in range(width // pair):
         q_t = wq_ref[:, t * pair : (t + 1) * pair].astype(F32)
@@ -107,21 +190,6 @@
         second = jnp.where(low, pltpu.roll(q_t, head_dim, 1), v_t)
         wh[:, 2 * t * pair : (2 * t + 1) * pair] = first.astype(BF16)
         wh[:, (2 * t + 1) * pair : (2 * t + 2) * pair] = second.astype(BF16)
-
-    pl.semaphore_wait(barrier, len(OFFSETS) + len(order))
-
-    z_copies = []
-    for kind, offset in enumerate(OFFSETS):
-        copy = pltpu.make_async_remote_copy(
-            src_ref=xb,
-            dst_ref=zrecv.at[pl.ds(kind * per_dev, per_dev)],
-            send_sem=z_send_sem.at[kind],
-            recv_sem=z_recv_sem.at[kind],
-            device_id=(img_peer(-offset), me),
-            device_id_type=MESH,
-        )
-        copy.start()
-        z_copies.append(copy)
 
     def spread(phase, send, recv):
         for offset in order:
@@ -154,14 +222,19 @@
         projected_heads(xb[image], own_send, image)
     spread(0, own_send, own_recv)
 
-    def kind_of(entry, home):
-        away = lax.rem(lax.div(entry, per_dev) - home + 2 * img_count, img_count)
-        return jnp.where(
-            away == 1, 0, jnp.where(away == img_count - 1, 1, jnp.where(away == 2, 2, 3))
-        )
-
-    my_entries = [partners[block * edges + e] for e in range(edges)]
-    my_kinds = [kind_of(entry, block) for entry in my_entries]
+    my_entries = entries_of(block)
+    my_slots = []
+    positions = [jnp.int32(0)] * edges
+    for kind, offset in enumerate(OFFSETS):
+        found, slots = slots_between(my_entries, img_peer(offset))
+        my_slots.append([edge for edge, _ in slots])
+        for e, (inside, rank) in enumerate(found):
+            positions[e] = jnp.where(
+                inside, kind * CAP + jnp.minimum(rank, CAP - 1), positions[e]
+            )
+    loads[1].wait()
+    for load in loads[5:]:
+        load.wait()
 
     hid[...] = (
         jnp.dot(
@@ -183,9 +256,7 @@
         copy.wait()
     for j in range(2):
         for image in range(per_dev):
-            e = 2 * image + j
-            at = my_kinds[e] * per_dev + lax.rem(my_entries[e], per_dev)
-            projected_heads(zrecv[at], part_send.at[j], image)
+            projected_heads(zrecv[positions[2 * image + j]], part_send.at[j], image)
         spread(1 + j, part_send.at[j], part_recv.at[j])
 
     chunk = min(256, keypoints)
@@ -225,7 +296,7 @@
     prepare(own_recv, counts[block * per_dev + my_image], k_own, v_own)
     for j in range(2):
         arrived(1 + j, part_send.at[j], part_recv.at[j])
-        asked = partners[block * edges + 2 * my_image + j]
+        asked = partners[j, block * per_dev + my_image]
         prepare(part_recv.at[j], counts[asked], k_part, v_part)
 
         def to_partner(c, n, message, j=j):
@@ -242,24 +313,12 @@
         attend(own_recv, k_part, v_part, to_own)
     spread(5, ret_send.at[2], sum_recv)
 
-    def ranks_of(kinds):
-        ranks = []
-        for e in range(edges):
-            rank = jnp.int32(0)
-            for before in range(e):
-                rank = rank + jnp.where(kinds[before] == kinds[e], 1, 0)
-            ranks.append(rank)
-        return ranks
-
-    my_ranks = ranks_of(my_kinds)
     arrived(3, ret_send.at[0], msg_recv.at[0])
     arrived(4, ret_send.at[1], msg_recv.at[1])
     back_copies = []
     for kind, offset in enumerate(OFFSETS):
         for c in range(CAP):
-            edge = jnp.int32(0)
-            for e in range(edges):
-                edge = edge + jnp.where((my_kinds[e] == kind) & (my_ranks[e] == c), e, 0)
+            edge = jnp.maximum(my_slots[kind][c] - 1, 0)
             image, j = lax.div(edge, 2), lax.rem(edge, 2)
             back_send[kind, c] = msg_recv[j, pl.ds(image * heads, heads)]
         copy = pltpu.make_async_remote_copy(
@@ -273,27 +332,6 @@
         copy.start()
         back_copies.append(copy)
 
-    weights = []
-    for kind, offset in enumerate(OFFSETS):
-        source = img_peer(-offset)
-        entries = [partners[source * edges + e] for e in range(edges)]
-        kinds = [kind_of(entry, source) for entry in entries]
-        ranks = ranks_of(kinds)
-        for c in range(CAP):
-            row = []
-            for image in range(per_dev):
-                hit = jnp.int32(0)
-                for e in range(edges):
-                    hit = hit + jnp.where(
-                        (kinds[e] == kind)
-                        & (ranks[e] == c)
-                        & (lax.rem(entries[e], per_dev) == image),
-                        1,
-                        0,
-                    )
-                row.append(hit)
-            weights.append(row)
-
     arrived(5, ret_send.at[2], sum_recv)
     for copy in back_copies:
         copy.wait()
@@ -304,7 +342,7 @@
         degree = jnp.int32(2)
         for kind in range(len(OFFSETS)):
             for c in range(CAP):
-                hit = weights[kind * CAP + c][image]
+                hit = jnp.where(incoming_slots[kind][c] == image + 1, 1, 0)
                 degree = degree + hit
                 inbox = inbox + hit.astype(F32) * back_recv[kind, c].astype(F32)
         packed.append((inbox / degree.astype(F32)).astype(BF16))
@@ -318,6 +356,7 @@
         proj[image * rows : image * rows + half, :] = mine[:, 0:width]
         proj[image * rows + half : (image + 1) * rows, :] = mine[:, width : 2 * width]
 
+    stores = []
     for image in range(per_dev):
         part = pl.ds(image * rows, rows)
         hidden = hid[part, :] + jnp.dot(
@@ -333,6 +372,10 @@
             + jnp.dot(active, f2_ref[...], preferred_element_type=F32)
             + b2_ref[...]
         )
+        stores.append(
+            pltpu.make_async_copy(out_ref.at[image], out_hbm.at[image], out_sem.at[image])
+        )
+        stores[-1].start()
 
     for phase, send in (
         (0, own_send),
@@ -343,6 +386,8 @@
         (5, ret_send.at[2]),
     ):
         left(phase, send)
+    for store in stores:
+        store.wait()
 
 
 def HEADS_OF(width):
@@ -373,19 +418,34 @@
     hidden = ffn_in.shape[1]
     half = rows // 2
     kinds = len(OFFSETS)
-    vmem = pl.BlockSpec(memory_space=pltpu.VMEM)
-    smem = pl.BlockSpec(memory_space=pltpu.SMEM)
+    anywhere = pl.BlockSpec(memory_space=pl.ANY)
     return pl.pallas_call(
         functools.partial(kernel, img_count, row_devices),
         out_shape=jax.ShapeDtypeStruct(features.shape, F32),
-        in_specs=[smem, smem] + [vmem] * 10,
-        out_specs=vmem,
+        in_specs=[anywhere] * 12,
+        out_specs=anywhere,
         scratch_shapes=[
+            pltpu.SMEM(partners.shape[::-1], jnp.int32),
+            pltpu.SMEM(counts.shape, jnp.int32),
+            pltpu.VMEM(features.shape, F32),
+            pltpu.VMEM(shared_proj.shape, BF16),
+            pltpu.VMEM(value_proj.shape, BF16),
+            pltpu.VMEM(out_proj.shape, BF16),
+            pltpu.VMEM(ffn_in.shape, BF16),
+            pltpu.VMEM((1, hidden), F32),
+            pltpu.VMEM((1, hidden), F32),
+            pltpu.VMEM((1, hidden), F32),
+            pltpu.VMEM(ffn_out.shape, BF16),
+            pltpu.VMEM((1, width), F32),
+            pltpu.VMEM(features.shape, F32),
+            pltpu.SemaphoreType.DMA((12,)),
+            pltpu.SemaphoreType.DMA((per_dev,)),
             pltpu.VMEM((per_dev, rows, width), BF16),
+            pltpu.VMEM((kinds, CAP, rows, width), BF16),
             pltpu.VMEM((width, 2 * width), BF16),
             pltpu.VMEM((heads * pair, 2 * width), BF16),
             pltpu.VMEM((per_dev * rows, hidden), F32),
-            pltpu.VMEM((kinds * per_dev, rows, width), BF16),
+            pltpu.VMEM((kinds * CAP, rows, width), BF16),
             pltpu.VMEM((row_devices, rows, pair), BF16),
             pltpu.VMEM((row_devices, rows, pair), BF16),
             pltpu.VMEM((2, row_devices, rows, pair), BF16),
@@ -410,10 +470,10 @@
             pltpu.SemaphoreType.DMA((kinds,)),
         ],
         compiler_params=pltpu.CompilerParams(
-            collective_id=0, has_side_effects=True, vmem_limit_bytes=48 * 1024 * 1024
+            collective_id=0, has_side_effects=True, vmem_limit_bytes=60 * 1024 * 1024
         ),
     )(
-        partners.reshape(-1),
+        partners.T,
         counts,
         features,
         shared_proj,

time: 54.7 us -> 48.6 us (0.89)
  local copies, waits for them, and re-layouts: 6.97 us -> 1.67 us
  Pallas kernels: 47.4 us -> 46.7 us
    unnamed x24 -> x1, local copies, waits for them, and re-layouts: 6.83 us -> 1.67 us
    pallas_call x1, Pallas kernels: 47.4 us -> 46.7 us  [per_device(): pl.pallas_call(functools.partial(kernel, img_count, row_devices), out_sha...]
where the time goes in v2:
time: 48.6 us; the launch traced here: 48.4 us
  Pallas kernels  46.7 us (96%)
  local copies, waits for them, and re-layouts  1.67 us (3%)
    pallas_call x1, Pallas kernels, per_device(): pl.pallas_call(functools.partial(kernel, img_count, row_devices), out_sha...  46.7 us
    unnamed x1, local copies, waits for them, and re-layouts  1.67 us

profile of v2, /device:TPU:1, one launch (start us, length us, event | category | flops | bytes accessed | tf_op | source)
XLA Modules:
  0.0 48.4 jit_solution(2558673192055669999)
XLA Ops:
  0.0 46.7 %shard_map.118 = f32[4,64,256]{2,1,0:T(8,128)} custom-call(s32[2,128]{1,0:T(2,128)} %bitcast.8, s32[128]{0:T(128)} %counts_hbm.1, f32[4,64,256]{2,1,0:T(8,128)} %x_hbm.1, bf16[256,256]{1,0:T(8,128)(2,1)} %wq_hbm.1, bf16[256,256]{1,0:T(8,128)(2,1)} %wv_hbm.1, bf16[256,256]{1,0:T(8,128)(2,1)} %wo_hbm.1, bf16[512,512]{1,0:T(8,128)(2,1)} %f1_hbm.1, ...), custom_call_target="tpu_custom_call" | custom-call | tf_op jit(solution)/shard_map/pallas_call | solution.py:422
  46.8 1.7 %copy.14 = f32[4,64,256]{2,1,0:T(8,128)} copy(f32[4,64,256]{2,1,0:T(8,128)} %shard_map.118) | data formatting | bytes 524288

commit v3 on v2

--- a/solution.py
+++ b/solution.py
@@ -68,9 +68,13 @@
     part_send,
     part_recv,
     k_own,
+    q_own,
     v_own,
     k_part,
+    q_part,
     v_part,
+    ahead_even,
+    ahead_odd,
     ret_acc,
     ret_send,
     msg_recv,
@@ -97,6 +101,7 @@
     block = lax.axis_index("img")
     me = lax.axis_index("row")
     my_image = lax.div(me, heads)
+    ahead = (ahead_even, ahead_odd)
     order = peer_order(row_devices)
 
     def img_peer(offset):
@@ -260,57 +265,64 @@
         spread(1 + j, part_send.at[j], part_recv.at[j])
 
     chunk = min(256, keypoints)
+    per_chunk = chunk // rows
     lane = lanes((keypoints, pair))
     place = lax.broadcasted_iota(jnp.int32, (keypoints, pair), 0)
-
-    def prepare(source, count, k_ref, v_ref):
-        flat = source[...].reshape(keypoints, pair).astype(F32)
+    level = lax.broadcasted_iota(jnp.int32, (pair, keypoints), 0)
+
+    def prepare(source, count, k_ref, q_ref, v_ref):
+        flat = source[...].reshape(keypoints, pair)
         penalty = jnp.where((lane == head_dim) & (place >= count), PENALTY, 0.0)
-        k_ref[...] = jnp.where(lane < head_dim, flat * scale, penalty).astype(BF16).T
-        v_ref[...] = jnp.where(
-            lane >= head_dim, flat, jnp.where(lane == 0, 1.0, 0.0)
-        ).astype(BF16)
-
-    def attend(asking, k_ref, v_ref, finish):
-        per_chunk = chunk // rows
-        low_chunk = lanes((chunk, pair)) < head_dim
+        k_ref[...] = jnp.where(lane < head_dim, flat.astype(F32) * scale, penalty).astype(BF16)
+        turned = flat.T
+        one = jnp.ones((), BF16)
+        q_ref[...] = jnp.where(level < head_dim, turned, one)
+        v_ref[...] = jnp.where(level < head_dim, one, turned)
+
+    def attend(work):
         low_half = lanes((chunk // 2, pair)) < head_dim
-
-        def one_chunk(c, carry):
-            q = asking[pl.ds(c * per_chunk, per_chunk)].reshape(chunk, pair)
-            q = jnp.where(low_chunk, q, jnp.ones((), BF16))
-            scores = jnp.dot(q, k_ref[...], preferred_element_type=F32)
-            peak = jnp.max(scores, axis=1, keepdims=True)
+        steps = [(job, c) for job in work for c in range(keypoints // chunk)]
+
+        def score(n):
+            (k_ref, q_ref, _, _), c = steps[n]
+            ahead[n % 2][...] = jnp.dot(
+                k_ref[...], q_ref[:, c * chunk : (c + 1) * chunk], preferred_element_type=F32
+            )
+
+        score(0)
+        for n, ((_, _, v_ref, finish), c) in enumerate(steps):
+            if n + 1 < len(steps):
+                score(n + 1)
+            scores = ahead[n % 2][...]
+            peak = jnp.max(scores, axis=0, keepdims=True)
             raised = jnp.exp(scores - peak).astype(BF16)
-            total = jnp.dot(raised, v_ref[...], preferred_element_type=F32)
-            message = total / total[:, 0:1]
+            total = jnp.dot(v_ref[...], raised, preferred_element_type=F32)
+            message = (total / total[0:1, :]).T
             split = message.reshape(per_chunk, 2, half, pair)
             upper = split[:, 0].reshape(chunk // 2, pair)
             lower = pltpu.roll(split[:, 1].reshape(chunk // 2, pair), head_dim, 1)
-            finish(c, per_chunk, jnp.where(low_half, lower, upper).reshape(per_chunk, half, pair))
-            return carry
-
-        lax.fori_loop(0, keypoints // chunk, one_chunk, 0)
+            finish(c, jnp.where(low_half, lower, upper).reshape(per_chunk, half, pair))
 
     arrived(0, own_send, own_recv)
-    prepare(own_recv, counts[block * per_dev + my_image], k_own, v_own)
+    prepare(own_recv, counts[block * per_dev + my_image], k_own, q_own, v_own)
     for j in range(2):
         arrived(1 + j, part_send.at[j], part_recv.at[j])
         asked = partners[j, block * per_dev + my_image]
-        prepare(part_recv.at[j], counts[asked], k_part, v_part)
-
-        def to_partner(c, n, message, j=j):
-            ret_send[j, pl.ds(c * n, n)] = message.astype(BF16)
-
-        def to_own(c, n, message, j=j):
+        prepare(part_recv.at[j], counts[asked], k_part, q_part, v_part)
+
+        def to_partner(c, message, j=j):
+            ret_send[j, c * per_chunk : (c + 1) * per_chunk] = message.astype(BF16)
+            if (c + 1) * chunk == keypoints:
+                spread(3 + j, ret_send.at[j], msg_recv.at[j])
+
+        def to_own(c, message, j=j):
+            part = slice(c * per_chunk, (c + 1) * per_chunk)
             if j == 0:
-                ret_acc[pl.ds(c * n, n)] = message
+                ret_acc[part] = message
             else:
-                ret_send[2, pl.ds(c * n, n)] = (ret_acc[pl.ds(c * n, n)] + message).astype(BF16)
-
-        attend(part_recv.at[j], k_own, v_own, to_partner)
-        spread(3 + j, ret_send.at[j], msg_recv.at[j])
-        attend(own_recv, k_part, v_part, to_own)
+                ret_send[2, part] = (ret_acc[part] + message).astype(BF16)
+
+        attend(((k_own, q_part, v_own, to_partner), (k_part, q_own, v_part, to_own)))
     spread(5, ret_send.at[2], sum_recv)
 
     arrived(3, ret_send.at[0], msg_recv.at[0])
@@ -450,10 +462,14 @@
             pltpu.VMEM((row_devices, rows, pair), BF16),
             pltpu.VMEM((2, row_devices, rows, pair), BF16),
             pltpu.VMEM((2, row_devices, rows, pair), BF16),
+            pltpu.VMEM((keypoints, pair), BF16),
+            pltpu.VMEM((pair, keypoints), BF16),
             pltpu.VMEM((pair, keypoints), BF16),
             pltpu.VMEM((keypoints, pair), BF16),
             pltpu.VMEM((pair, keypoints), BF16),
-            pltpu.VMEM((keypoints, pair), BF16),
+            pltpu.VMEM((pair, keypoints), BF16),
+            pltpu.VMEM((keypoints, min(256, keypoints)), F32),
+            pltpu.VMEM((keypoints, min(256, keypoints)), F32),
             pltpu.VMEM((row_devices, half, pair), F32),
             pltpu.VMEM((3, row_devices, half, pair), BF16),
             pltpu.VMEM((2, row_devices, half, pair), BF16),

time: 48.6 us -> 45.3 us (0.932)
  Pallas kernels: 46.7 us -> 43.1 us
    pallas_call x1, Pallas kernels: 46.7 us -> 43.1 us  [per_device(): pl.pallas_call(functools.partial(kernel, img_count, row_devices), out_sha...]
where the time goes in v3:
time: 45.3 us; the launch traced here: 44.8 us
  Pallas kernels  43.1 us (95%)
  local copies, waits for them, and re-layouts  1.67 us (4%)
    pallas_call x1, Pallas kernels, per_device(): pl.pallas_call(functools.partial(kernel, img_count, row_devices), out_sha...  43.1 us
    unnamed x1, local copies, waits for them, and re-layouts  1.67 us

profile of v3, /device:TPU:1, one launch (start us, length us, event | category | flops | bytes accessed | tf_op | source)
XLA Modules:
  0.0 44.8 jit_solution(4337111579878154709)
XLA Ops:
  0.0 43.1 %shard_map.118 = f32[4,64,256]{2,1,0:T(8,128)} custom-call(s32[2,128]{1,0:T(2,128)} %bitcast.8, s32[128]{0:T(128)} %counts_hbm.1, f32[4,64,256]{2,1,0:T(8,128)} %x_hbm.1, bf16[256,256]{1,0:T(8,128)(2,1)} %wq_hbm.1, bf16[256,256]{1,0:T(8,128)(2,1)} %wv_hbm.1, bf16[256,256]{1,0:T(8,128)(2,1)} %wo_hbm.1, bf16[512,512]{1,0:T(8,128)(2,1)} %f1_hbm.1, ...), custom_call_target="tpu_custom_call" | custom-call | tf_op jit(solution)/shard_map/pallas_call | solution.py:434
  43.1 1.7 %copy.14 = f32[4,64,256]{2,1,0:T(8,128)} copy(f32[4,64,256]{2,1,0:T(8,128)} %shard_map.118) | data formatting | bytes 524288

commit v4 on v3

--- a/solution.py
+++ b/solution.py
@@ -16,10 +16,8 @@
 BF16 = jnp.bfloat16
 
 
-def peer_order(count):
-    if count == 16:
-        return (1, 4, 15, 12, 5, 11, 3, 13, 2, 8, 6, 9, 14, 7, 10)
-    return tuple(range(1, count))
+def far_first(count):
+    return sorted(range(count), key=lambda step: (-min(step, count - step), step))
 
 
 def lanes(shape):
@@ -101,14 +99,20 @@
     block = lax.axis_index("img")
     me = lax.axis_index("row")
     my_image = lax.div(me, heads)
+    my_head = lax.rem(me, heads)
     ahead = (ahead_even, ahead_odd)
-    order = peer_order(row_devices)
+    rings = far_first(per_dev)
 
     def img_peer(offset):
         return lax.rem(block + (offset + img_count), img_count)
 
-    def row_peer(offset):
-        return lax.rem(me + offset, row_devices)
+    def image_at(dy):
+        return lax.rem(my_image + dy, per_dev)
+
+    def line(dy):
+        for dx in far_first(heads):
+            if dy or dx:
+                yield image_at(dy) * heads + lax.rem(my_head + dx, heads)
 
     loads = [
         pltpu.make_async_copy(source, target, in_sem.at[n])
@@ -135,10 +139,9 @@
     barrier = pltpu.get_barrier_semaphore()
     for offset in OFFSETS:
         pl.semaphore_signal(barrier, inc=1, device_id=(img_peer(offset), me), device_id_type=MESH)
-    for offset in order:
-        pl.semaphore_signal(
-            barrier, inc=1, device_id=(block, row_peer(offset)), device_id_type=MESH
-        )
+    for dy in rings:
+        for peer in line(dy):
+            pl.semaphore_signal(barrier, inc=1, device_id=(block, peer), device_id_type=MESH)
 
     def entries_of(home):
         return [partners[e % 2, home * per_dev + e // 2] for e in range(edges)]
@@ -170,7 +173,7 @@
         for c in range(CAP):
             zsend[kind, c] = xb[jnp.maximum(incoming_slots[kind][c] - 1, 0)]
 
-    pl.semaphore_wait(barrier, len(OFFSETS) + len(order))
+    pl.semaphore_wait(barrier, len(OFFSETS) + row_devices - 1)
 
     z_copies = []
     for kind, offset in enumerate(OFFSETS):
@@ -196,9 +199,8 @@
         wh[:, 2 * t * pair : (2 * t + 1) * pair] = first.astype(BF16)
         wh[:, (2 * t + 1) * pair : (2 * t + 2) * pair] = second.astype(BF16)
 
-    def spread(phase, send, recv):
-        for offset in order:
-            peer = row_peer(offset)
+    def spread(phase, send, recv, dy):
+        for peer in line(dy):
             pltpu.make_async_remote_copy(
                 src_ref=send.at[peer],
                 dst_ref=recv.at[me],
@@ -207,7 +209,8 @@
                 device_id=(block, peer),
                 device_id_type=MESH,
             ).start()
-        pltpu.make_async_copy(send.at[me], recv.at[me], l_sem.at[phase]).start()
+        if dy == 0:
+            pltpu.make_async_copy(send.at[me], recv.at[me], l_sem.at[phase]).start()
 
     def arrived(phase, send, recv):
         rest = pl.ds(0, row_devices - 1)
@@ -223,9 +226,10 @@
         for h in range(heads):
             send[image * heads + h] = both[:, h * pair : (h + 1) * pair]
 
-    for image in range(per_dev):
+    for dy in rings:
+        image = image_at(dy)
         projected_heads(xb[image], own_send, image)
-    spread(0, own_send, own_recv)
+        spread(0, own_send, own_recv, dy)
 
     my_entries = entries_of(block)
     my_slots = []
@@ -260,12 +264,15 @@
     for copy in z_copies:
         copy.wait()
     for j in range(2):
-        for image in range(per_dev):
-            projected_heads(zrecv[positions[2 * image + j]], part_send.at[j], image)
-        spread(1 + j, part_send.at[j], part_recv.at[j])
-
-    chunk = min(256, keypoints)
-    per_chunk = chunk // rows
+        for dy in rings:
+            image = image_at(dy)
+            at = positions[j]
+            for other in range(1, per_dev):
+                at = jnp.where(image == other, positions[2 * other + j], at)
+            projected_heads(zrecv[at], part_send.at[j], image)
+            spread(1 + j, part_send.at[j], part_recv.at[j], dy)
+
+    chunk = rows * heads
     lane = lanes((keypoints, pair))
     place = lax.broadcasted_iota(jnp.int32, (keypoints, pair), 0)
     level = lax.broadcasted_iota(jnp.int32, (pair, keypoints), 0)
@@ -281,16 +288,17 @@
 
     def attend(work):
         low_half = lanes((chunk // 2, pair)) < head_dim
-        steps = [(job, c) for job in work for c in range(keypoints // chunk)]
+        steps = [(job, dy) for job in work for dy in rings]
 
         def score(n):
-            (k_ref, q_ref, _, _), c = steps[n]
+            (k_ref, q_ref, _, _), dy = steps[n]
+            part = pl.ds(pl.multiple_of(image_at(dy) * chunk, chunk), chunk)
             ahead[n % 2][...] = jnp.dot(
-                k_ref[...], q_ref[:, c * chunk : (c + 1) * chunk], preferred_element_type=F32
+                k_ref[...], q_ref[:, part], preferred_element_type=F32
             )
 
         score(0)
-        for n, ((_, _, v_ref, finish), c) in enumerate(steps):
+        for n, ((_, _, v_ref, finish), dy) in enumerate(steps):
             if n + 1 < len(steps):
                 score(n + 1)
             scores = ahead[n % 2][...]
@@ -298,10 +306,10 @@
             raised = jnp.exp(scores - peak).astype(BF16)
             total = jnp.dot(v_ref[...], raised, preferred_element_type=F32)
             message = (total / total[0:1, :]).T
-            split = message.reshape(per_chunk, 2, half, pair)
+            split = message.reshape(heads, 2, half, pair)
             upper = split[:, 0].reshape(chunk // 2, pair)
             lower = pltpu.roll(split[:, 1].reshape(chunk // 2, pair), head_dim, 1)
-            finish(c, jnp.where(low_half, lower, upper).reshape(per_chunk, half, pair))
+            finish(dy, jnp.where(low_half, lower, upper).reshape(heads, half, pair))
 
     arrived(0, own_send, own_recv)
     prepare(own_recv, counts[block * per_dev + my_image], k_own, q_own, v_own)
@@ -310,20 +318,19 @@
         asked = partners[j, block * per_dev + my_image]
         prepare(part_recv.at[j], counts[asked], k_part, q_part, v_part)
 
-        def to_partner(c, message, j=j):
-            ret_send[j, c * per_chunk : (c + 1) * per_chunk] = message.astype(BF16)
-            if (c + 1) * chunk == keypoints:
-                spread(3 + j, ret_send.at[j], msg_recv.at[j])
-
-        def to_own(c, message, j=j):
-            part = slice(c * per_chunk, (c + 1) * per_chunk)
+        def to_partner(dy, message, j=j):
+            ret_send[j, pl.ds(image_at(dy) * heads, heads)] = message.astype(BF16)
+            spread(3 + j, ret_send.at[j], msg_recv.at[j], dy)
+
+        def to_own(dy, message, j=j):
+            part = pl.ds(image_at(dy) * heads, heads)
             if j == 0:
                 ret_acc[part] = message
             else:
                 ret_send[2, part] = (ret_acc[part] + message).astype(BF16)
+                spread(5, ret_send.at[2], sum_recv, dy)
 
         attend(((k_own, q_part, v_own, to_partner), (k_part, q_own, v_part, to_own)))
-    spread(5, ret_send.at[2], sum_recv)
 
     arrived(3, ret_send.at[0], msg_recv.at[0])
     arrived(4, ret_send.at[1], msg_recv.at[1])
@@ -380,9 +387,7 @@
         normed = away * lax.rsqrt(spreads + 1e-5) * gain_ref[...] + nbias_ref[...]
         active = (0.5 * normed * (1.0 + lax.erf(normed * (0.5**0.5)))).astype(BF16)
         out_ref[image] = (
-            x_ref[image]
-            + jnp.dot(active, f2_ref[...], preferred_element_type=F32)
-            + b2_ref[...]
+            jnp.dot(active, f2_ref[...], preferred_element_type=F32) + b2_ref[...]
         )
         stores.append(
             pltpu.make_async_copy(out_ref.at[image], out_hbm.at[image], out_sem.at[image])
@@ -431,7 +436,7 @@
     half = rows // 2
     kinds = len(OFFSETS)
     anywhere = pl.BlockSpec(memory_space=pl.ANY)
-    return pl.pallas_call(
+    update = pl.pallas_call(
         functools.partial(kernel, img_count, row_devices),
         out_shape=jax.ShapeDtypeStruct(features.shape, F32),
         in_specs=[anywhere] * 12,
@@ -468,8 +473,8 @@
             pltpu.VMEM((keypoints, pair), BF16),
             pltpu.VMEM((pair, keypoints), BF16),
             pltpu.VMEM((pair, keypoints), BF16),
-            pltpu.VMEM((keypoints, min(256, keypoints)), F32),
-            pltpu.VMEM((keypoints, min(256, keypoints)), F32),
+            pltpu.VMEM((keypoints, rows * heads), F32),
+            pltpu.VMEM((keypoints, rows * heads), F32),
             pltpu.VMEM((row_devices, half, pair), F32),
             pltpu.VMEM((3, row_devices, half, pair), BF16),
             pltpu.VMEM((2, row_devices, half, pair), BF16),
@@ -502,6 +507,7 @@
         ffn_out,
         ffn_out_bias.reshape(1, -1),
     )
+    return features + update
 
 
 def solution(mesh):

time: 45.3 us -> 46.1 us (1.018)
  other arithmetic: 0 us -> 1.69 us
  local copies, waits for them, and re-layouts: 1.67 us -> 0.01 us
  Pallas kernels: 43.1 us -> 44.3 us
    add x0 -> x1, other arithmetic: none -> 1.69 us  [per_device(): return features + update]
    unnamed x1 -> x2, local copies, waits for them, and re-layouts: 1.67 us -> 0.01 us
    pallas_call x1, Pallas kernels: 43.1 us -> 44.3 us  [per_device(): pl.pallas_call(functools.partial(kernel, img_count, row_devices), out_sha...]
where the time goes in v4:
time: 46.1 us; the launch traced here: 46 us
  Pallas kernels  44.3 us (96%)
  other arithmetic  1.69 us (4%)
    pallas_call x1, Pallas kernels, per_device(): pl.pallas_call(functools.partial(kernel, img_count, row_devices), out_sha...  44.3 us
    add x1, other arithmetic, per_device(): return features + update  1.69 us

profile of v4, /device:TPU:1, one launch (start us, length us, event | category | flops | bytes accessed | tf_op | source)
XLA Modules:
  0.0 46.0 jit_solution(9463364749913376974)
XLA Ops:
  0.0 0.0 copy-start
  0.0 44.3 %shard_map.118 = f32[4,64,256]{2,1,0:T(8,128)} custom-call(s32[2,128]{1,0:T(2,128)} %bitcast.8, s32[128]{0:T(128)} %counts_hbm.1, f32[4,64,256]{2,1,0:T(8,128)} %x_hbm.1, bf16[256,256]{1,0:T(8,128)(2,1)} %wq_hbm.1, bf16[256,256]{1,0:T(8,128)(2,1)} %wv_hbm.1, bf16[256,256]{1,0:T(8,128)(2,1)} %wo_hbm.1, bf16[512,512]{1,0:T(8,128)(2,1)} %f1_hbm.1, ...), custom_call_target="tpu_custom_call" | custom-call | tf_op jit(solution)/shard_map/pallas_call | solution.py:439
  44.3 0.0 copy-done
  44.3 1.7 %add.3 = f32[4,64,256]{2,1,0:T(8,128)} add(f32[4,64,256]{2,1,0:T(8,128)S(1)} %copy-done, f32[4,64,256]{2,1,0:T(8,128)} %shard_map.118) | non-fusion elementwise | flops 65536 | bytes 786432 | tf_op jit(solution)/shard_map/add | solution.py:510
Async XLA Ops:
  0.0 44.3 %copy-start = (f32[4,64,256]{2,1,0:T(8,128)S(1)}, f32[4,64,256]{2,1,0:T(8,128)}, u32[]{:S(2)}) copy-start(f32[4,64,256]{2,1,0:T(8,128)} %x_hbm.1) | copy-start | bytes 786436

commit v5 on v4

--- a/solution.py
+++ b/solution.py
@@ -69,7 +69,6 @@
     q_own,
     v_own,
     k_part,
-    q_part,
     v_part,
     ahead_even,
     ahead_odd,
@@ -84,6 +83,7 @@
     z_recv_sem,
     a_send_sem,
     a_recv_sem,
+    p_recv_sem,
     l_sem,
     b_send_sem,
     b_recv_sem,
@@ -205,7 +205,9 @@
                 src_ref=send.at[peer],
                 dst_ref=recv.at[me],
                 send_sem=a_send_sem.at[phase],
-                recv_sem=a_recv_sem.at[phase],
+                recv_sem=(
+                    p_recv_sem.at[phase - 1, dy] if phase in (1, 2) else a_recv_sem.at[phase]
+                ),
                 device_id=(block, peer),
                 device_id_type=MESH,
             ).start()
@@ -273,56 +275,62 @@
             spread(1 + j, part_send.at[j], part_recv.at[j], dy)
 
     chunk = rows * heads
-    lane = lanes((keypoints, pair))
-    place = lax.broadcasted_iota(jnp.int32, (keypoints, pair), 0)
-    level = lax.broadcasted_iota(jnp.int32, (pair, keypoints), 0)
-
-    def prepare(source, count, k_ref, q_ref, v_ref):
-        flat = source[...].reshape(keypoints, pair)
+    def as_keys(flat, first, count):
+        place = first + lax.broadcasted_iota(jnp.int32, flat.shape, 0)
+        lane = lanes(flat.shape)
         penalty = jnp.where((lane == head_dim) & (place >= count), PENALTY, 0.0)
-        k_ref[...] = jnp.where(lane < head_dim, flat.astype(F32) * scale, penalty).astype(BF16)
-        turned = flat.T
+        return jnp.where(lane < head_dim, flat.astype(F32) * scale, penalty).astype(BF16)
+
+    def turned(flat):
+        across = flat.T
+        level = lax.broadcasted_iota(jnp.int32, across.shape, 0)
         one = jnp.ones((), BF16)
-        q_ref[...] = jnp.where(level < head_dim, turned, one)
-        v_ref[...] = jnp.where(level < head_dim, one, turned)
-
-    def attend(work):
-        low_half = lanes((chunk // 2, pair)) < head_dim
-        steps = [(job, dy) for job in work for dy in rings]
-
-        def score(n):
-            (k_ref, q_ref, _, _), dy = steps[n]
-            part = pl.ds(pl.multiple_of(image_at(dy) * chunk, chunk), chunk)
-            ahead[n % 2][...] = jnp.dot(
-                k_ref[...], q_ref[:, part], preferred_element_type=F32
-            )
-
-        score(0)
-        for n, ((_, _, v_ref, finish), dy) in enumerate(steps):
-            if n + 1 < len(steps):
-                score(n + 1)
-            scores = ahead[n % 2][...]
-            peak = jnp.max(scores, axis=0, keepdims=True)
-            raised = jnp.exp(scores - peak).astype(BF16)
-            total = jnp.dot(v_ref[...], raised, preferred_element_type=F32)
-            message = (total / total[0:1, :]).T
-            split = message.reshape(heads, 2, half, pair)
-            upper = split[:, 0].reshape(chunk // 2, pair)
-            lower = pltpu.roll(split[:, 1].reshape(chunk // 2, pair), head_dim, 1)
-            finish(dy, jnp.where(low_half, lower, upper).reshape(heads, half, pair))
-
-    arrived(0, own_send, own_recv)
-    prepare(own_recv, counts[block * per_dev + my_image], k_own, q_own, v_own)
-    for j in range(2):
-        arrived(1 + j, part_send.at[j], part_recv.at[j])
-        asked = partners[j, block * per_dev + my_image]
-        prepare(part_recv.at[j], counts[asked], k_part, q_part, v_part)
-
-        def to_partner(dy, message, j=j):
-            ret_send[j, pl.ds(image_at(dy) * heads, heads)] = message.astype(BF16)
-            spread(3 + j, ret_send.at[j], msg_recv.at[j], dy)
-
-        def to_own(dy, message, j=j):
+        return jnp.where(level < head_dim, across, one), jnp.where(level < head_dim, one, across)
+
+    def line_arrived(j, dy):
+        count = heads if dy else heads - 1
+        rest = part_recv.at[j].at[pl.ds(0, count)]
+        pltpu.make_async_copy(rest, rest, p_recv_sem.at[j, dy]).wait()
+        if dy == 0:
+            pltpu.make_async_copy(
+                part_send.at[j].at[me], part_recv.at[j].at[me], l_sem.at[1 + j]
+            ).wait()
+
+    def score(n):
+        side, j, dy = steps[n]
+        if side == "partner":
+            line_arrived(j, dy)
+            source = image_at(per_dev - dy)
+            place = pl.ds(pl.multiple_of(source * chunk, chunk), chunk)
+            flat = part_recv[j, pl.ds(source * heads, heads)].reshape(chunk, pair)
+            k_part[j, place, :] = as_keys(flat, source * chunk, asked_counts[j])
+            queries, values = turned(flat)
+            v_part[j, :, place] = values
+            keys = k_own[...]
+        else:
+            place = pl.ds(pl.multiple_of(image_at(dy) * chunk, chunk), chunk)
+            queries = q_own[:, place]
+            keys = k_part[j]
+        ahead[n % 2][...] = jnp.dot(keys, queries, preferred_element_type=F32)
+
+    low_half = lanes((chunk // 2, pair)) < head_dim
+
+    def attend(n):
+        side, j, dy = steps[n]
+        values = v_own[...] if side == "partner" else v_part[j]
+        scores = ahead[n % 2][...]
+        peak = jnp.max(scores, axis=0, keepdims=True)
+        raised = jnp.exp(scores - peak).astype(BF16)
+        total = jnp.dot(values, raised, preferred_element_type=F32)
+        split = (total / total[0:1, :]).T.reshape(heads, 2, half, pair)
+        upper = split[:, 0].reshape(chunk // 2, pair)
+        lower = pltpu.roll(split[:, 1].reshape(chunk // 2, pair), head_dim, 1)
+        message = jnp.where(low_half, lower, upper).reshape(heads, half, pair)
+        if side == "partner":
+            ahead_by = (per_dev - dy) % per_dev
+            ret_send[j, pl.ds(image_at(ahead_by) * heads, heads)] = message.astype(BF16)
+            spread(3 + j, ret_send.at[j], msg_recv.at[j], ahead_by)
+        else:
             part = pl.ds(image_at(dy) * heads, heads)
             if j == 0:
                 ret_acc[part] = message
@@ -330,7 +338,19 @@
                 ret_send[2, part] = (ret_acc[part] + message).astype(BF16)
                 spread(5, ret_send.at[2], sum_recv, dy)
 
-        attend(((k_own, q_part, v_own, to_partner), (k_part, q_own, v_part, to_own)))
+    steps = [(side, j, dy) for side in ("partner", "own") for j in range(2) for dy in rings]
+    asked_counts = [counts[partners[j, block * per_dev + my_image]] for j in range(2)]
+    arrived(0, own_send, own_recv)
+    whole = own_recv[...].reshape(keypoints, pair)
+    k_own[...] = as_keys(whole, 0, counts[block * per_dev + my_image])
+    own_queries, own_values = turned(whole)
+    q_own[...] = own_queries
+    v_own[...] = own_values
+    score(0)
+    for n in range(len(steps)):
+        if n + 1 < len(steps):
+            score(n + 1)
+        attend(n)
 
     arrived(3, ret_send.at[0], msg_recv.at[0])
     arrived(4, ret_send.at[1], msg_recv.at[1])
@@ -470,9 +490,8 @@
             pltpu.VMEM((keypoints, pair), BF16),
             pltpu.VMEM((pair, keypoints), BF16),
             pltpu.VMEM((pair, keypoints), BF16),
-            pltpu.VMEM((keypoints, pair), BF16),
-            pltpu.VMEM((pair, keypoints), BF16),
-            pltpu.VMEM((pair, keypoints), BF16),
+            pltpu.VMEM((2, keypoints, pair), BF16),
+            pltpu.VMEM((2, pair, keypoints), BF16),
             pltpu.VMEM((keypoints, rows * heads), F32),
             pltpu.VMEM((keypoints, rows * heads), F32),
             pltpu.VMEM((row_devices, half, pair), F32),
@@ -486,6 +505,7 @@
             pltpu.SemaphoreType.DMA((kinds,)),
             pltpu.SemaphoreType.DMA((6,)),
             pltpu.SemaphoreType.DMA((6,)),
+            pltpu.SemaphoreType.DMA((2, per_dev)),
             pltpu.SemaphoreType.DMA((6,)),
             pltpu.SemaphoreType.DMA((kinds,)),
             pltpu.SemaphoreType.DMA((kinds,)),

time: 46.1 us -> 44 us (0.954)
  Pallas kernels: 44.3 us -> 42.1 us
    pallas_call x1, Pallas kernels: 44.3 us -> 42.1 us  [per_device(): pl.pallas_call(functools.partial(kernel, img_count, row_devices), out_sha...]
where the time goes in v5:
time: 44 us; the launch traced here: 43.8 us
  Pallas kernels  42.1 us (96%)
  other arithmetic  1.69 us (4%)
    pallas_call x1, Pallas kernels, per_device(): pl.pallas_call(functools.partial(kernel, img_count, row_devices), out_sha...  42.1 us
    add x1, other arithmetic, per_device(): return features + update  1.69 us

profile of v5, /device:TPU:1, one launch (start us, length us, event | category | flops | bytes accessed | tf_op | source)
XLA Modules:
  0.0 43.8 jit_solution(10272727021824334700)
XLA Ops:
  0.0 0.0 copy-start
  0.0 42.1 %shard_map.118 = f32[4,64,256]{2,1,0:T(8,128)} custom-call(s32[2,128]{1,0:T(2,128)} %bitcast.8, s32[128]{0:T(128)} %counts_hbm.1, f32[4,64,256]{2,1,0:T(8,128)} %x_hbm.1, bf16[256,256]{1,0:T(8,128)(2,1)} %wq_hbm.1, bf16[256,256]{1,0:T(8,128)(2,1)} %wv_hbm.1, bf16[256,256]{1,0:T(8,128)(2,1)} %wo_hbm.1, bf16[512,512]{1,0:T(8,128)(2,1)} %f1_hbm.1, ...), custom_call_target="tpu_custom_call" | custom-call | tf_op jit(solution)/shard_map/pallas_call | solution.py:459
  42.1 0.0 copy-done
  42.1 1.7 %add.3 = f32[4,64,256]{2,1,0:T(8,128)} add(f32[4,64,256]{2,1,0:T(8,128)S(1)} %copy-done, f32[4,64,256]{2,1,0:T(8,128)} %shard_map.118) | non-fusion elementwise | flops 65536 | bytes 786432 | tf_op jit(solution)/shard_map/add | solution.py:530
Async XLA Ops:
  0.0 42.1 %copy-start = (f32[4,64,256]{2,1,0:T(8,128)S(1)}, f32[4,64,256]{2,1,0:T(8,128)}, u32[]{:S(2)}) copy-start(f32[4,64,256]{2,1,0:T(8,128)} %x_hbm.1) | copy-start | bytes 786436

commit v6 on v5

--- a/solution.py
+++ b/solution.py
@@ -60,7 +60,8 @@
     wh,
     w2,
     hid,
-    zrecv,
+    zrecv_first,
+    zrecv_second,
     own_send,
     own_recv,
     part_send,
@@ -102,6 +103,7 @@
     my_head = lax.rem(me, heads)
     ahead = (ahead_even, ahead_odd)
     rings = far_first(per_dev)
+    zrecv = (zrecv_first, zrecv_second)
 
     def img_peer(offset):
         return lax.rem(block + (offset + img_count), img_count)
@@ -169,24 +171,28 @@
         incoming_slots.append([image for _, image in slots])
     loads[2].wait()
     xb[...] = x_ref[...].astype(BF16)
-    for kind in range(len(OFFSETS)):
-        for c in range(CAP):
-            zsend[kind, c] = xb[jnp.maximum(incoming_slots[kind][c] - 1, 0)]
+    for part in range(2):
+        for kind in range(len(OFFSETS)):
+            for c in range(CAP):
+                zsend[part, kind, c] = xb[
+                    jnp.maximum(incoming_slots[kind][c] - 1, 0), part * half : (part + 1) * half
+                ]
 
     pl.semaphore_wait(barrier, len(OFFSETS) + row_devices - 1)
 
     z_copies = []
-    for kind, offset in enumerate(OFFSETS):
-        copy = pltpu.make_async_remote_copy(
-            src_ref=zsend.at[kind],
-            dst_ref=zrecv.at[pl.ds(kind * CAP, CAP)],
-            send_sem=z_send_sem.at[kind],
-            recv_sem=z_recv_sem.at[kind],
-            device_id=(img_peer(-offset), me),
-            device_id_type=MESH,
-        )
-        copy.start()
-        z_copies.append(copy)
+    for part in range(2):
+        for kind, offset in enumerate(OFFSETS):
+            copy = pltpu.make_async_remote_copy(
+                src_ref=zsend.at[part, kind],
+                dst_ref=zrecv[part].at[pl.ds(kind * CAP, CAP)],
+                send_sem=z_send_sem.at[part, kind],
+                recv_sem=z_recv_sem.at[part, kind],
+                device_id=(img_peer(-offset), me),
+                device_id_type=MESH,
+            )
+            copy.start()
+            z_copies.append(copy)
 
     loads[3].wait()
     loads[4].wait()
@@ -199,11 +205,14 @@
         wh[:, 2 * t * pair : (2 * t + 1) * pair] = first.astype(BF16)
         wh[:, (2 * t + 1) * pair : (2 * t + 2) * pair] = second.astype(BF16)
 
-    def spread(phase, send, recv, dy):
+    def spread(phase, send, recv, dy, rows_of=None):
+        def block_of(ref, which):
+            return ref.at[which] if rows_of is None else ref.at[which, rows_of]
+
         for peer in line(dy):
             pltpu.make_async_remote_copy(
-                src_ref=send.at[peer],
-                dst_ref=recv.at[me],
+                src_ref=block_of(send, peer),
+                dst_ref=block_of(recv, me),
                 send_sem=a_send_sem.at[phase],
                 recv_sem=(
                     p_recv_sem.at[phase - 1, dy] if phase in (1, 2) else a_recv_sem.at[phase]
@@ -212,7 +221,9 @@
                 device_id_type=MESH,
             ).start()
         if dy == 0:
-            pltpu.make_async_copy(send.at[me], recv.at[me], l_sem.at[phase]).start()
+            pltpu.make_async_copy(
+                block_of(send, me), block_of(recv, me), l_sem.at[phase]
+            ).start()
 
     def arrived(phase, send, recv):
         rest = pl.ds(0, row_devices - 1)
@@ -223,14 +234,14 @@
         rest = pl.ds(0, row_devices - 1)
         pltpu.make_async_copy(send.at[rest], send.at[rest], a_send_sem.at[phase]).wait()
 
-    def projected_heads(source, send, image):
+    def projected_heads(source, send, image, rows_of):
         both = jnp.dot(source, wh[...], preferred_element_type=F32).astype(BF16)
         for h in range(heads):
-            send[image * heads + h] = both[:, h * pair : (h + 1) * pair]
+            send[image * heads + h, rows_of] = both[:, h * pair : (h + 1) * pair]
 
     for dy in rings:
         image = image_at(dy)
-        projected_heads(xb[image], own_send, image)
+        projected_heads(xb[image], own_send, image, pl.ds(0, rows))
         spread(0, own_send, own_recv, dy)
 
     my_entries = entries_of(block)
@@ -263,16 +274,18 @@
         w2[h * pair + head_dim : (h + 1) * pair, 0:width] = piece
         w2[h * pair + head_dim : (h + 1) * pair, width : 2 * width] = blank
 
-    for copy in z_copies:
-        copy.wait()
-    for j in range(2):
-        for dy in rings:
-            image = image_at(dy)
-            at = positions[j]
-            for other in range(1, per_dev):
-                at = jnp.where(image == other, positions[2 * other + j], at)
-            projected_heads(zrecv[at], part_send.at[j], image)
-            spread(1 + j, part_send.at[j], part_recv.at[j], dy)
+    for part in range(2):
+        for kind in range(len(OFFSETS)):
+            z_copies[part * len(OFFSETS) + kind].wait_recv()
+        rows_of = pl.ds(part * half, half)
+        for j in range(2):
+            for dy in rings:
+                image = image_at(dy)
+                at = positions[j]
+                for other in range(1, per_dev):
+                    at = jnp.where(image == other, positions[2 * other + j], at)
+                projected_heads(zrecv[part][at], part_send.at[j], image, rows_of)
+                spread(1 + j, part_send.at[j], part_recv.at[j], dy, rows_of)
 
     chunk = rows * heads
     def as_keys(flat, first, count):
@@ -372,19 +385,24 @@
         back_copies.append(copy)
 
     arrived(5, ret_send.at[2], sum_recv)
-    for copy in back_copies:
-        copy.wait()
-
-    packed = []
+    inboxes, degrees = [], []
     for image in range(per_dev):
-        inbox = sum_recv[image * heads : (image + 1) * heads].astype(F32)
+        inboxes.append(sum_recv[image * heads : (image + 1) * heads].astype(F32))
         degree = jnp.int32(2)
-        for kind in range(len(OFFSETS)):
-            for c in range(CAP):
-                hit = jnp.where(incoming_slots[kind][c] == image + 1, 1, 0)
-                degree = degree + hit
-                inbox = inbox + hit.astype(F32) * back_recv[kind, c].astype(F32)
-        packed.append((inbox / degree.astype(F32)).astype(BF16))
+        for slots in incoming_slots:
+            for slot in slots:
+                degree = degree + jnp.where(slot == image + 1, 1, 0)
+        degrees.append(degree.astype(F32))
+    for kind in range(len(OFFSETS)):
+        back_copies[kind].wait_recv()
+        for c in range(CAP):
+            message = back_recv[kind, c].astype(F32)
+            for image in range(per_dev):
+                hit = jnp.where(incoming_slots[kind][c] == image + 1, 1.0, 0.0)
+                inboxes[image] = inboxes[image] + hit * message
+    packed = [
+        (inbox / degree).astype(BF16) for inbox, degree in zip(inboxes, degrees, strict=True)
+    ]
     stacked = jnp.concatenate(
         [jnp.concatenate([packed[i][h] for i in range(per_dev)], axis=0) for h in range(heads)],
         axis=1,
@@ -423,6 +441,8 @@
         (5, ret_send.at[2]),
     ):
         left(phase, send)
+    for copy in z_copies + back_copies:
+        copy.wait_send()
     for store in stores:
         store.wait()
 
@@ -478,11 +498,12 @@
             pltpu.SemaphoreType.DMA((12,)),
             pltpu.SemaphoreType.DMA((per_dev,)),
             pltpu.VMEM((per_dev, rows, width), BF16),
-            pltpu.VMEM((kinds, CAP, rows, width), BF16),
+            pltpu.VMEM((2, kinds, CAP, half, width), BF16),
             pltpu.VMEM((width, 2 * width), BF16),
             pltpu.VMEM((heads * pair, 2 * width), BF16),
             pltpu.VMEM((per_dev * rows, hidden), F32),
-            pltpu.VMEM((kinds * CAP, rows, width), BF16),
+            pltpu.VMEM((kinds * CAP, half, width), BF16),
+            pltpu.VMEM((kinds * CAP, half, width), BF16),
             pltpu.VMEM((row_devices, rows, pair), BF16),
             pltpu.VMEM((row_devices, rows, pair), BF16),
             pltpu.VMEM((2, row_devices, rows, pair), BF16),
@@ -501,8 +522,8 @@
             pltpu.VMEM((kinds, CAP, heads, half, pair), BF16),
             pltpu.VMEM((kinds, CAP, heads, half, pair), BF16),
             pltpu.VMEM((per_dev * rows, width), BF16),
-            pltpu.SemaphoreType.DMA((kinds,)),
-            pltpu.SemaphoreType.DMA((kinds,)),
+            pltpu.SemaphoreType.DMA((2, kinds)),
+            pltpu.SemaphoreType.DMA((2, kinds)),
             pltpu.SemaphoreType.DMA((6,)),
             pltpu.SemaphoreType.DMA((6,)),
             pltpu.SemaphoreType.DMA((2, per_dev)),

time: 44 us -> 43.3 us (0.984)
  Pallas kernels: 42.1 us -> 41.2 us
    pallas_call x1, Pallas kernels: 42.1 us -> 41.2 us  [per_device(): pl.pallas_call(functools.partial(kernel, img_count, row_devices), out_sha...]
where the time goes in v6:
time: 43.3 us; the launch traced here: 42.9 us
  Pallas kernels  41.2 us (95%)
  other arithmetic  1.69 us (4%)
    pallas_call x1, Pallas kernels, per_device(): pl.pallas_call(functools.partial(kernel, img_count, row_devices), out_sha...  41.2 us
    add x1, other arithmetic, per_device(): return features + update  1.69 us

profile of v6, /device:TPU:1, one launch (start us, length us, event | category | flops | bytes accessed | tf_op | source)
XLA Modules:
  0.0 42.9 jit_solution(11323011706438556813)
XLA Ops:
  0.0 0.0 copy-start
  0.0 41.2 %shard_map.118 = f32[4,64,256]{2,1,0:T(8,128)} custom-call(s32[2,128]{1,0:T(2,128)} %bitcast.8, s32[128]{0:T(128)} %counts_hbm.1, f32[4,64,256]{2,1,0:T(8,128)} %x_hbm.1, bf16[256,256]{1,0:T(8,128)(2,1)} %wq_hbm.1, bf16[256,256]{1,0:T(8,128)(2,1)} %wv_hbm.1, bf16[256,256]{1,0:T(8,128)(2,1)} %wo_hbm.1, bf16[512,512]{1,0:T(8,128)(2,1)} %f1_hbm.1, ...), custom_call_target="tpu_custom_call" | custom-call | tf_op jit(solution)/shard_map/pallas_call | solution.py:479
  41.2 0.0 copy-done
  41.2 1.7 %add.3 = f32[4,64,256]{2,1,0:T(8,128)} add(f32[4,64,256]{2,1,0:T(8,128)S(1)} %copy-done, f32[4,64,256]{2,1,0:T(8,128)} %shard_map.118) | non-fusion elementwise | flops 65536 | bytes 786432 | tf_op jit(solution)/shard_map/add | solution.py:551
Async XLA Ops:
  0.0 41.2 %copy-start = (f32[4,64,256]{2,1,0:T(8,128)S(1)}, f32[4,64,256]{2,1,0:T(8,128)}, u32[]{:S(2)}) copy-start(f32[4,64,256]{2,1,0:T(8,128)} %x_hbm.1) | copy-start | bytes 786436

commit v7 on v6

--- a/solution.py
+++ b/solution.py
@@ -215,7 +215,7 @@
                 dst_ref=block_of(recv, me),
                 send_sem=a_send_sem.at[phase],
                 recv_sem=(
-                    p_recv_sem.at[phase - 1, dy] if phase in (1, 2) else a_recv_sem.at[phase]
+                    p_recv_sem.at[dy] if phase == 1 else a_recv_sem.at[phase]
                 ),
                 device_id=(block, peer),
                 device_id_type=MESH,
@@ -274,55 +274,70 @@
         w2[h * pair + head_dim : (h + 1) * pair, 0:width] = piece
         w2[h * pair + head_dim : (h + 1) * pair, width : 2 * width] = blank
 
+    low_rows = lanes((half, pair)) < head_dim
     for part in range(2):
         for kind in range(len(OFFSETS)):
             z_copies[part * len(OFFSETS) + kind].wait_recv()
         rows_of = pl.ds(part * half, half)
-        for j in range(2):
-            for dy in rings:
-                image = image_at(dy)
+        for dy in rings:
+            image = image_at(dy)
+            sides = []
+            for j in range(2):
                 at = positions[j]
                 for other in range(1, per_dev):
                     at = jnp.where(image == other, positions[2 * other + j], at)
-                projected_heads(zrecv[part][at], part_send.at[j], image, rows_of)
-                spread(1 + j, part_send.at[j], part_recv.at[j], dy, rows_of)
+                sides.append(jnp.dot(zrecv[part][at], wh[...], preferred_element_type=F32))
+            for h in range(heads):
+                one, two = (side[:, h * pair : (h + 1) * pair] for side in sides)
+                keys = jnp.where(low_rows, one, pltpu.roll(two, head_dim, 1))
+                values = jnp.where(low_rows, pltpu.roll(one, head_dim, 1), two)
+                part_send[0, image * heads + h, rows_of] = keys.astype(BF16)
+                part_send[1, image * heads + h, rows_of] = values.astype(BF16)
+            spread(1, part_send.at[0], part_recv.at[0], dy, rows_of)
+    for part in range(2):
+        for dy in rings:
+            spread(2, part_send.at[1], part_recv.at[1], dy, pl.ds(part * half, half))
 
     chunk = rows * heads
-    def as_keys(flat, first, count):
+    def as_keys(flat, first, count, upper):
         place = first + lax.broadcasted_iota(jnp.int32, flat.shape, 0)
         lane = lanes(flat.shape)
-        penalty = jnp.where((lane == head_dim) & (place >= count), PENALTY, 0.0)
-        return jnp.where(lane < head_dim, flat.astype(F32) * scale, penalty).astype(BF16)
-
-    def turned(flat):
-        across = flat.T
-        level = lax.broadcasted_iota(jnp.int32, across.shape, 0)
-        one = jnp.ones((), BF16)
-        return jnp.where(level < head_dim, across, one), jnp.where(level < head_dim, one, across)
-
-    def line_arrived(j, dy):
+        inside = (lane >= head_dim) if upper else (lane < head_dim)
+        penalty = jnp.where((lane == (0 if upper else head_dim)) & (place >= count), PENALTY, 0.0)
+        return jnp.where(inside, flat.astype(F32) * scale, penalty).astype(BF16)
+
+    def beside_ones(across, upper):
+        ones = jnp.ones(across.shape, BF16)
+        return jnp.concatenate([ones, across] if upper else [across, ones], axis=0)
+
+    def line_arrived(dy):
         count = heads if dy else heads - 1
-        rest = part_recv.at[j].at[pl.ds(0, count)]
-        pltpu.make_async_copy(rest, rest, p_recv_sem.at[j, dy]).wait()
+        rest = part_recv.at[0].at[pl.ds(0, count)]
+        pltpu.make_async_copy(rest, rest, p_recv_sem.at[dy]).wait()
         if dy == 0:
             pltpu.make_async_copy(
-                part_send.at[j].at[me], part_recv.at[j].at[me], l_sem.at[1 + j]
+                part_send.at[0].at[me], part_recv.at[0].at[me], l_sem.at[1]
             ).wait()
 
     def score(n):
         side, j, dy = steps[n]
         if side == "partner":
-            line_arrived(j, dy)
+            if j == 0:
+                line_arrived(dy)
             source = image_at(per_dev - dy)
             place = pl.ds(pl.multiple_of(source * chunk, chunk), chunk)
-            flat = part_recv[j, pl.ds(source * heads, heads)].reshape(chunk, pair)
-            k_part[j, place, :] = as_keys(flat, source * chunk, asked_counts[j])
-            queries, values = turned(flat)
-            v_part[j, :, place] = values
+            flat = part_recv[0, pl.ds(source * heads, heads)].reshape(chunk, pair)
+            k_part[j, place, :] = as_keys(flat, source * chunk, asked_counts[j], j == 1)
+            queries = beside_ones(flat.T[j * head_dim : (j + 1) * head_dim], False)
             keys = k_own[...]
         else:
+            if j == 0 and dy == rings[0]:
+                arrived(2, part_send.at[1], part_recv.at[1])
+                across = part_recv[1].reshape(keypoints, pair).T
+                v_part[0] = beside_ones(across[0:head_dim], True)
+                v_part[1] = beside_ones(across[head_dim:pair], True)
             place = pl.ds(pl.multiple_of(image_at(dy) * chunk, chunk), chunk)
-            queries = q_own[:, place]
+            queries = q_own[j, :, place]
             keys = k_part[j]
         ahead[n % 2][...] = jnp.dot(keys, queries, preferred_element_type=F32)
 
@@ -351,14 +366,16 @@
                 ret_send[2, part] = (ret_acc[part] + message).astype(BF16)
                 spread(5, ret_send.at[2], sum_recv, dy)
 
-    steps = [(side, j, dy) for side in ("partner", "own") for j in range(2) for dy in rings]
+    steps = [("partner", j, dy) for dy in rings for j in range(2)]
+    steps += [("own", j, dy) for j in range(2) for dy in rings]
     asked_counts = [counts[partners[j, block * per_dev + my_image]] for j in range(2)]
     arrived(0, own_send, own_recv)
     whole = own_recv[...].reshape(keypoints, pair)
-    k_own[...] = as_keys(whole, 0, counts[block * per_dev + my_image])
-    own_queries, own_values = turned(whole)
-    q_own[...] = own_queries
-    v_own[...] = own_values
+    k_own[...] = as_keys(whole, 0, counts[block * per_dev + my_image], False)
+    across = whole.T
+    q_own[0] = beside_ones(across[0:head_dim], False)
+    q_own[1] = beside_ones(across[0:head_dim], True)
+    v_own[...] = beside_ones(across[head_dim:pair], True)
     score(0)
     for n in range(len(steps)):
         if n + 1 < len(steps):
@@ -509,7 +526,7 @@
             pltpu.VMEM((2, row_devices, rows, pair), BF16),
             pltpu.VMEM((2, row_devices, rows, pair), BF16),
             pltpu.VMEM((keypoints, pair), BF16),
-            pltpu.VMEM((pair, keypoints), BF16),
+            pltpu.VMEM((2, pair, keypoints), BF16),
             pltpu.VMEM((pair, keypoints), BF16),
             pltpu.VMEM((2, keypoints, pair), BF16),
             pltpu.VMEM((2, pair, keypoints), BF16),
@@ -526,7 +543,7 @@
             pltpu.SemaphoreType.DMA((2, kinds)),
             pltpu.SemaphoreType.DMA((6,)),
             pltpu.SemaphoreType.DMA((6,)),
-            pltpu.SemaphoreType.DMA((2, per_dev)),
+            pltpu.SemaphoreType.DMA((per_dev,)),
             pltpu.SemaphoreType.DMA((6,)),
             pltpu.SemaphoreType.DMA((kinds,)),
             pltpu.SemaphoreType.DMA((kinds,)),

time: 43.3 us -> 42.4 us (0.979)
  Pallas kernels: 41.2 us -> 40.6 us
    pallas_call x1, Pallas kernels: 41.2 us -> 40.6 us  [per_device(): pl.pallas_call(functools.partial(kernel, img_count, row_devices), out_sha...]
where the time goes in v7:
time: 42.4 us; the launch traced here: 42.3 us
  Pallas kernels  40.6 us (96%)
  other arithmetic  1.69 us (4%)
    pallas_call x1, Pallas kernels, per_device(): pl.pallas_call(functools.partial(kernel, img_count, row_devices), out_sha...  40.6 us
    add x1, other arithmetic, per_device(): return features + update  1.69 us

profile of v7, /device:TPU:1, one launch (start us, length us, event | category | flops | bytes accessed | tf_op | source)
XLA Modules:
  0.0 42.3 jit_solution(5327783937265047932)
XLA Ops:
  0.0 0.0 copy-start
  0.0 40.6 %shard_map.118 = f32[4,64,256]{2,1,0:T(8,128)} custom-call(s32[2,128]{1,0:T(2,128)} %bitcast.8, s32[128]{0:T(128)} %counts_hbm.1, f32[4,64,256]{2,1,0:T(8,128)} %x_hbm.1, bf16[256,256]{1,0:T(8,128)(2,1)} %wq_hbm.1, bf16[256,256]{1,0:T(8,128)(2,1)} %wv_hbm.1, bf16[256,256]{1,0:T(8,128)(2,1)} %wo_hbm.1, bf16[512,512]{1,0:T(8,128)(2,1)} %f1_hbm.1, ...), custom_call_target="tpu_custom_call" | custom-call | tf_op jit(solution)/shard_map/pallas_call | solution.py:496
  40.6 0.0 copy-done
  40.6 1.7 %add.3 = f32[4,64,256]{2,1,0:T(8,128)} add(f32[4,64,256]{2,1,0:T(8,128)S(1)} %copy-done, f32[4,64,256]{2,1,0:T(8,128)} %shard_map.118) | non-fusion elementwise | flops 65536 | bytes 786432 | tf_op jit(solution)/shard_map/add | solution.py:568
Async XLA Ops:
  0.0 40.6 %copy-start = (f32[4,64,256]{2,1,0:T(8,128)S(1)}, f32[4,64,256]{2,1,0:T(8,128)}, u32[]{:S(2)}) copy-start(f32[4,64,256]{2,1,0:T(8,128)} %x_hbm.1) | copy-start | bytes 786436

commit v8 on v7

--- a/solution.py
+++ b/solution.py
@@ -74,7 +74,8 @@
     ahead_even,
     ahead_odd,
     ret_acc,
-    ret_send,
+    msg_send,
+    sum_send,
     msg_recv,
     sum_recv,
     back_send,
@@ -294,9 +295,8 @@
                 part_send[0, image * heads + h, rows_of] = keys.astype(BF16)
                 part_send[1, image * heads + h, rows_of] = values.astype(BF16)
             spread(1, part_send.at[0], part_recv.at[0], dy, rows_of)
-    for part in range(2):
-        for dy in rings:
-            spread(2, part_send.at[1], part_recv.at[1], dy, pl.ds(part * half, half))
+    for dy in rings:
+        spread(2, part_send.at[1], part_recv.at[1], dy)
 
     chunk = rows * heads
     def as_keys(flat, first, count, upper):
@@ -356,15 +356,16 @@
         message = jnp.where(low_half, lower, upper).reshape(heads, half, pair)
         if side == "partner":
             ahead_by = (per_dev - dy) % per_dev
-            ret_send[j, pl.ds(image_at(ahead_by) * heads, heads)] = message.astype(BF16)
-            spread(3 + j, ret_send.at[j], msg_recv.at[j], ahead_by)
+            msg_send[pl.ds(image_at(ahead_by) * heads, heads), j] = message.astype(BF16)
+            if j == 1:
+                spread(3, msg_send, msg_recv, ahead_by)
         else:
             part = pl.ds(image_at(dy) * heads, heads)
             if j == 0:
                 ret_acc[part] = message
             else:
-                ret_send[2, part] = (ret_acc[part] + message).astype(BF16)
-                spread(5, ret_send.at[2], sum_recv, dy)
+                sum_send[part] = (ret_acc[part] + message).astype(BF16)
+                spread(4, sum_send, sum_recv, dy)
 
     steps = [("partner", j, dy) for dy in rings for j in range(2)]
     steps += [("own", j, dy) for j in range(2) for dy in rings]
@@ -382,14 +383,13 @@
             score(n + 1)
         attend(n)
 
-    arrived(3, ret_send.at[0], msg_recv.at[0])
-    arrived(4, ret_send.at[1], msg_recv.at[1])
+    arrived(3, msg_send, msg_recv)
     back_copies = []
     for kind, offset in enumerate(OFFSETS):
         for c in range(CAP):
             edge = jnp.maximum(my_slots[kind][c] - 1, 0)
             image, j = lax.div(edge, 2), lax.rem(edge, 2)
-            back_send[kind, c] = msg_recv[j, pl.ds(image * heads, heads)]
+            back_send[kind, c] = msg_recv[pl.ds(image * heads, heads), j]
         copy = pltpu.make_async_remote_copy(
             src_ref=back_send.at[kind],
             dst_ref=back_recv.at[kind],
@@ -401,7 +401,7 @@
         copy.start()
         back_copies.append(copy)
 
-    arrived(5, ret_send.at[2], sum_recv)
+    arrived(4, sum_send, sum_recv)
     inboxes, degrees = [], []
     for image in range(per_dev):
         inboxes.append(sum_recv[image * heads : (image + 1) * heads].astype(F32))
@@ -453,9 +453,8 @@
         (0, own_send),
         (1, part_send.at[0]),
         (2, part_send.at[1]),
-        (3, ret_send.at[0]),
-        (4, ret_send.at[1]),
-        (5, ret_send.at[2]),
+        (3, msg_send),
+        (4, sum_send),
     ):
         left(phase, send)
     for copy in z_copies + back_copies:
@@ -533,18 +532,19 @@
             pltpu.VMEM((keypoints, rows * heads), F32),
             pltpu.VMEM((keypoints, rows * heads), F32),
             pltpu.VMEM((row_devices, half, pair), F32),
-            pltpu.VMEM((3, row_devices, half, pair), BF16),
-            pltpu.VMEM((2, row_devices, half, pair), BF16),
+            pltpu.VMEM((row_devices, 2, half, pair), BF16),
+            pltpu.VMEM((row_devices, half, pair), BF16),
+            pltpu.VMEM((row_devices, 2, half, pair), BF16),
             pltpu.VMEM((row_devices, half, pair), BF16),
             pltpu.VMEM((kinds, CAP, heads, half, pair), BF16),
             pltpu.VMEM((kinds, CAP, heads, half, pair), BF16),
             pltpu.VMEM((per_dev * rows, width), BF16),
             pltpu.SemaphoreType.DMA((2, kinds)),
             pltpu.SemaphoreType.DMA((2, kinds)),
-            pltpu.SemaphoreType.DMA((6,)),
-            pltpu.SemaphoreType.DMA((6,)),
+            pltpu.SemaphoreType.DMA((5,)),
+            pltpu.SemaphoreType.DMA((5,)),
             pltpu.SemaphoreType.DMA((per_dev,)),
-            pltpu.SemaphoreType.DMA((6,)),
+            pltpu.SemaphoreType.DMA((5,)),
             pltpu.SemaphoreType.DMA((kinds,)),
             pltpu.SemaphoreType.DMA((kinds,)),
         ],

time: 42.4 us -> 42.4 us (level)
  no operation moved by 1% of the time
where the time goes in v8:
time: 42.4 us; the launch traced here: 42.3 us
  Pallas kernels  40.6 us (96%)
  other arithmetic  1.69 us (4%)
    pallas_call x1, Pallas kernels, per_device(): pl.pallas_call(functools.partial(kernel, img_count, row_devices), out_sha...  40.6 us
    add x1, other arithmetic, per_device(): return features + update  1.69 us

profile of v8, /device:TPU:1, one launch (start us, length us, event | category | flops | bytes accessed | tf_op | source)
XLA Modules:
  0.0 42.3 jit_solution(16947799344669635075)
XLA Ops:
  0.0 0.0 copy-start
  0.0 40.6 %shard_map.118 = f32[4,64,256]{2,1,0:T(8,128)} custom-call(s32[2,128]{1,0:T(2,128)} %bitcast.8, s32[128]{0:T(128)} %counts_hbm.1, f32[4,64,256]{2,1,0:T(8,128)} %x_hbm.1, bf16[256,256]{1,0:T(8,128)(2,1)} %wq_hbm.1, bf16[256,256]{1,0:T(8,128)(2,1)} %wv_hbm.1, bf16[256,256]{1,0:T(8,128)(2,1)} %wo_hbm.1, bf16[512,512]{1,0:T(8,128)(2,1)} %f1_hbm.1, ...), custom_call_target="tpu_custom_call" | custom-call | tf_op jit(solution)/shard_map/pallas_call | solution.py:495
  40.6 0.0 copy-done
  40.6 1.7 %add.3 = f32[4,64,256]{2,1,0:T(8,128)} add(f32[4,64,256]{2,1,0:T(8,128)S(1)} %copy-done, f32[4,64,256]{2,1,0:T(8,128)} %shard_map.118) | non-fusion elementwise | flops 65536 | bytes 786432 | tf_op jit(solution)/shard_map/add | solution.py:568
Async XLA Ops:
  0.0 40.6 %copy-start = (f32[4,64,256]{2,1,0:T(8,128)S(1)}, f32[4,64,256]{2,1,0:T(8,128)}, u32[]{:S(2)}) copy-start(f32[4,64,256]{2,1,0:T(8,128)} %x_hbm.1) | copy-start | bytes 786436

commit v9 on v8

--- a/solution.py
+++ b/solution.py
@@ -39,7 +39,10 @@
     nbias_hbm,
     f2_hbm,
     b2_hbm,
-    out_hbm,
+    out_0,
+    out_1,
+    out_2,
+    out_3,
     partners,
     counts,
     x_ref,
@@ -52,9 +55,7 @@
     nbias_ref,
     f2_ref,
     b2_ref,
-    out_ref,
     in_sem,
-    out_sem,
     xb,
     zsend,
     wh,
@@ -430,7 +431,7 @@
         proj[image * rows : image * rows + half, :] = mine[:, 0:width]
         proj[image * rows + half : (image + 1) * rows, :] = mine[:, width : 2 * width]
 
-    stores = []
+    outs = (out_0, out_1, out_2, out_3)
     for image in range(per_dev):
         part = pl.ds(image * rows, rows)
         hidden = hid[part, :] + jnp.dot(
@@ -441,13 +442,9 @@
         spreads = jnp.mean(away * away, axis=1, keepdims=True)
         normed = away * lax.rsqrt(spreads + 1e-5) * gain_ref[...] + nbias_ref[...]
         active = (0.5 * normed * (1.0 + lax.erf(normed * (0.5**0.5)))).astype(BF16)
-        out_ref[image] = (
+        outs[image][...] = (
             jnp.dot(active, f2_ref[...], preferred_element_type=F32) + b2_ref[...]
         )
-        stores.append(
-            pltpu.make_async_copy(out_ref.at[image], out_hbm.at[image], out_sem.at[image])
-        )
-        stores[-1].start()
 
     for phase, send in (
         (0, own_send),
@@ -459,8 +456,6 @@
         left(phase, send)
     for copy in z_copies + back_copies:
         copy.wait_send()
-    for store in stores:
-        store.wait()
 
 
 def HEADS_OF(width):
@@ -494,9 +489,9 @@
     anywhere = pl.BlockSpec(memory_space=pl.ANY)
     update = pl.pallas_call(
         functools.partial(kernel, img_count, row_devices),
-        out_shape=jax.ShapeDtypeStruct(features.shape, F32),
+        out_shape=[jax.ShapeDtypeStruct(features.shape[1:], F32)] * per_dev,
         in_specs=[anywhere] * 12,
-        out_specs=anywhere,
+        out_specs=[pl.BlockSpec(memory_space=pltpu.VMEM)] * per_dev,
         scratch_shapes=[
             pltpu.SMEM(partners.shape[::-1], jnp.int32),
             pltpu.SMEM(counts.shape, jnp.int32),
@@ -510,9 +505,7 @@
             pltpu.VMEM((1, hidden), F32),
             pltpu.VMEM(ffn_out.shape, BF16),
             pltpu.VMEM((1, width), F32),
-            pltpu.VMEM(features.shape, F32),
             pltpu.SemaphoreType.DMA((12,)),
-            pltpu.SemaphoreType.DMA((per_dev,)),
             pltpu.VMEM((per_dev, rows, width), BF16),
             pltpu.VMEM((2, kinds, CAP, half, width), BF16),
             pltpu.VMEM((width, 2 * width), BF16),
@@ -549,7 +542,7 @@
             pltpu.SemaphoreType.DMA((kinds,)),
         ],
         compiler_params=pltpu.CompilerParams(
-            collective_id=0, has_side_effects=True, vmem_limit_bytes=60 * 1024 * 1024
+            collective_id=0, has_side_effects=True, vmem_limit_bytes=67043328 - 10550 * 1024
         ),
     )(
         partners.T,
@@ -565,7 +558,7 @@
         ffn_out,
         ffn_out_bias.reshape(1, -1),
     )
-    return features + update
+    return features + jnp.stack(update)
 
 
 def solution(mesh):

time: 42.4 us -> 41.6 us (0.981)
  other arithmetic: 1.69 us -> 0.74 us
  local copies, waits for them, and re-layouts: 0.01 us -> 0.72 us
  Pallas kernels: 40.6 us -> 39.9 us
    add x1, other arithmetic: 1.69 us -> 0.74 us  [per_device(): return features + jnp.stack(update)]
    unnamed x2 -> x14, local copies, waits for them, and re-layouts: 0.01 us -> 0.72 us
    pallas_call x1, Pallas kernels: 40.6 us -> 39.9 us  [per_device(): pl.pallas_call(functools.partial(kernel, img_count, row_devices), out_sha...]
where the time goes in v9:
time: 41.6 us; the launch traced here: 41.4 us
  Pallas kernels  39.9 us (96%)
  other arithmetic  0.74 us (2%)
  local copies, waits for them, and re-layouts  0.72 us (2%)
    pallas_call x1, Pallas kernels, per_device(): pl.pallas_call(functools.partial(kernel, img_count, row_devices), out_sha...  39.9 us

profile of v9, /device:TPU:1, one launch (start us, length us, event | category | flops | bytes accessed | tf_op | source)
XLA Modules:
  0.0 41.4 jit_solution(17231265828037221189)
XLA Ops:
  0.0 0.0 copy-start.4
  0.0 0.0 copy-start.2
  0.0 0.0 copy-start.1
  0.0 0.0 copy-start
  0.0 0.0 copy-start.3
  0.0 0.0 copy-start.5
  0.0 0.6 %copy-done.4 = f32[256]{0:T(256)S(1)} copy-done((f32[256]{0:T(256)S(1)}, f32[256]{0:T(256)}, u32[]{:S(2)}) %copy-start.4) | copy-done | bytes 1048
  0.7 0.0 copy-done.2
  0.7 0.0 copy-done.1
  0.7 0.0 copy-done
  0.7 0.0 copy-done.3
  0.7 0.0 copy-done.5
  0.7 0.0 copy-start.6
  0.7 39.9 %shard_map.118 = (f32[64,256]{1,0:T(8,128)S(1)}, f32[64,256]{1,0:T(8,128)S(1)}, f32[64,256]{1,0:T(8,128)S(1)}, f32[64,256]{1,0:T(8,128)S(1)}) custom-call(s32[2,128]{1,0:T(2,128)S(1)} %bitcast.16, s32[128]{0:T(128)S(1)} %copy-done.5, f32[4,64,256]{2,1,0:T(8,128)} %x_hbm.1, bf16[256,256]{1,0:T(8,128)(2,1)} %wq_hbm.1, bf16[256,256]{1,0:T(8,128)(2,1)} %wv_hbm.1, ...), custom_call_target="tpu_custom_call" | custom-call | tf_op jit(solution)/shard_map/pallas_call | solution.py:490
  40.7 0.0 copy-done.6
  40.7 0.7 %maximum_add_fusion = f32[4,64,256]{2,1,0:T(8,128)} fusion(f32[4,64,256]{2,1,0:T(8,128)S(1)} %copy-done.6, f32[1,64,256]{2,1,0:T(8,128)S(1)} %bitcast.12, f32[1,64,256]{2,1,0:T(8,128)S(1)} %bitcast.11, f32[1,64,256]{2,1,0:T(8,128)S(1)} %bitcast.10, f32[1,64,256]{2,1,0:T(8,128)S(1)} %bitcast.9), kind=kLoop, calls=%fused_computation | loop fusion | flops 262144 | bytes 786432 | tf_op jit(solution)/shard_map/add | solution.py:561
Async XLA Ops:
  0.0 0.7 %copy-start.4 = (f32[256]{0:T(256)S(1)}, f32[256]{0:T(256)}, u32[]{:S(2)}) copy-start(f32[256]{0:T(256)} %param.23) | copy-start | bytes 3076
  0.0 0.7 %copy-start.2 = (f32[512]{0:T(512)S(1)}, f32[512]{0:T(512)}, u32[]{:S(2)}) copy-start(f32[512]{0:T(512)} %param.21) | copy-start | bytes 6148
  0.0 0.7 %copy-start.1 = (f32[512]{0:T(512)S(1)}, f32[512]{0:T(512)}, u32[]{:S(2)}) copy-start(f32[512]{0:T(512)} %param.20) | copy-start | bytes 6148
  0.0 0.7 %copy-start = (f32[512]{0:T(512)S(1)}, f32[512]{0:T(512)}, u32[]{:S(2)}) copy-start(f32[512]{0:T(512)} %param.19) | copy-start | bytes 6148
  0.0 0.7 %copy-start.3 = (s32[128,2]{0,1:T(2,128)S(1)}, s32[128,2]{0,1:T(2,128)}, u32[]{:S(2)}) copy-start(s32[128,2]{0,1:T(2,128)} %param.13) | copy-start | bytes 3076
  0.0 0.7 %copy-start.5 = (s32[128]{0:T(128)S(1)}, s32[128]{0:T(128)}, u32[]{:S(2)}) copy-start(s32[128]{0:T(128)} %counts_hbm.1) | copy-start | bytes 1540
  0.7 39.9 %copy-start.6 = (f32[4,64,256]{2,1,0:T(8,128)S(1)}, f32[4,64,256]{2,1,0:T(8,128)}, u32[]{:S(2)}) copy-start(f32[4,64,256]{2,1,0:T(8,128)} %x_hbm.1) | copy-start | bytes 786436

commit v10 on v9

--- a/solution.py
+++ b/solution.py
@@ -378,29 +378,33 @@
     q_own[0] = beside_ones(across[0:head_dim], False)
     q_own[1] = beside_ones(across[0:head_dim], True)
     v_own[...] = beside_ones(across[head_dim:pair], True)
+    back_copies = []
+
+    def send_back():
+        arrived(3, msg_send, msg_recv)
+        for kind, offset in enumerate(OFFSETS):
+            for c in range(CAP):
+                edge = jnp.maximum(my_slots[kind][c] - 1, 0)
+                image, j = lax.div(edge, 2), lax.rem(edge, 2)
+                back_send[kind, c] = msg_recv[pl.ds(image * heads, heads), j]
+            copy = pltpu.make_async_remote_copy(
+                src_ref=back_send.at[kind],
+                dst_ref=back_recv.at[kind],
+                send_sem=b_send_sem.at[kind],
+                recv_sem=b_recv_sem.at[kind],
+                device_id=(img_peer(offset), me),
+                device_id_type=MESH,
+            )
+            copy.start()
+            back_copies.append(copy)
+
     score(0)
     for n in range(len(steps)):
         if n + 1 < len(steps):
             score(n + 1)
         attend(n)
-
-    arrived(3, msg_send, msg_recv)
-    back_copies = []
-    for kind, offset in enumerate(OFFSETS):
-        for c in range(CAP):
-            edge = jnp.maximum(my_slots[kind][c] - 1, 0)
-            image, j = lax.div(edge, 2), lax.rem(edge, 2)
-            back_send[kind, c] = msg_recv[pl.ds(image * heads, heads), j]
-        copy = pltpu.make_async_remote_copy(
-            src_ref=back_send.at[kind],
-            dst_ref=back_recv.at[kind],
-            send_sem=b_send_sem.at[kind],
-            recv_sem=b_recv_sem.at[kind],
-            device_id=(img_peer(offset), me),
-            device_id_type=MESH,
-        )
-        copy.start()
-        back_copies.append(copy)
+        if n + 3 == len(steps):
+            send_back()
 
     arrived(4, sum_send, sum_recv)
     inboxes, degrees = [], []

time: 41.6 us -> 42.4 us (1.019)
  the two profiles are of different devices: /device:TPU:1 before, /device:TPU:2 now
where the time goes in v10:
time: 42.4 us; the launch traced here: 42.3 us
  Pallas kernels  40.8 us (96%)
  other arithmetic  0.74 us (2%)
  local copies, waits for them, and re-layouts  0.72 us (2%)
    pallas_call x1, Pallas kernels, per_device(): pl.pallas_call(functools.partial(kernel, img_count, row_devices), out_sha...  40.8 us

profile of v10, /device:TPU:2, one launch (start us, length us, event | category | flops | bytes accessed | tf_op | source)
XLA Modules:
  0.0 42.3 jit_solution(5729692089692449867)
XLA Ops:
  0.0 0.0 copy-start.4
  0.0 0.0 copy-start.2
  0.0 0.0 copy-start.1
  0.0 0.0 copy-start
  0.0 0.0 copy-start.3
  0.0 0.0 copy-start.5
  0.0 0.6 %copy-done.4 = f32[256]{0:T(256)S(1)} copy-done((f32[256]{0:T(256)S(1)}, f32[256]{0:T(256)}, u32[]{:S(2)}) %copy-start.4) | copy-done | bytes 1048
  0.7 0.0 copy-done.2
  0.7 0.0 copy-done.1
  0.7 0.0 copy-done
  0.7 0.0 copy-done.3
  0.7 0.0 copy-done.5
  0.7 0.0 copy-start.6
  0.7 40.8 %shard_map.118 = (f32[64,256]{1,0:T(8,128)S(1)}, f32[64,256]{1,0:T(8,128)S(1)}, f32[64,256]{1,0:T(8,128)S(1)}, f32[64,256]{1,0:T(8,128)S(1)}) custom-call(s32[2,128]{1,0:T(2,128)S(1)} %bitcast.16, s32[128]{0:T(128)S(1)} %copy-done.5, f32[4,64,256]{2,1,0:T(8,128)} %x_hbm.1, bf16[256,256]{1,0:T(8,128)(2,1)} %wq_hbm.1, bf16[256,256]{1,0:T(8,128)(2,1)} %wv_hbm.1, ...), custom_call_target="tpu_custom_call" | custom-call | tf_op jit(solution)/shard_map/pallas_call | solution.py:494
  41.5 0.0 copy-done.6
  41.6 0.7 %maximum_add_fusion = f32[4,64,256]{2,1,0:T(8,128)} fusion(f32[4,64,256]{2,1,0:T(8,128)S(1)} %copy-done.6, f32[1,64,256]{2,1,0:T(8,128)S(1)} %bitcast.12, f32[1,64,256]{2,1,0:T(8,128)S(1)} %bitcast.11, f32[1,64,256]{2,1,0:T(8,128)S(1)} %bitcast.10, f32[1,64,256]{2,1,0:T(8,128)S(1)} %bitcast.9), kind=kLoop, calls=%fused_computation | loop fusion | flops 262144 | bytes 786432 | tf_op jit(solution)/shard_map/add | solution.py:565
Async XLA Ops:
  0.0 0.7 %copy-start.4 = (f32[256]{0:T(256)S(1)}, f32[256]{0:T(256)}, u32[]{:S(2)}) copy-start(f32[256]{0:T(256)} %param.23) | copy-start | bytes 3076
  0.0 0.7 %copy-start.2 = (f32[512]{0:T(512)S(1)}, f32[512]{0:T(512)}, u32[]{:S(2)}) copy-start(f32[512]{0:T(512)} %param.21) | copy-start | bytes 6148
  0.0 0.7 %copy-start.1 = (f32[512]{0:T(512)S(1)}, f32[512]{0:T(512)}, u32[]{:S(2)}) copy-start(f32[512]{0:T(512)} %param.20) | copy-start | bytes 6148
  0.0 0.7 %copy-start = (f32[512]{0:T(512)S(1)}, f32[512]{0:T(512)}, u32[]{:S(2)}) copy-start(f32[512]{0:T(512)} %param.19) | copy-start | bytes 6148
  0.0 0.7 %copy-start.3 = (s32[128,2]{0,1:T(2,128)S(1)}, s32[128,2]{0,1:T(2,128)}, u32[]{:S(2)}) copy-start(s32[128,2]{0,1:T(2,128)} %param.13) | copy-start | bytes 3076
  0.0 0.7 %copy-start.5 = (s32[128]{0:T(128)S(1)}, s32[128]{0:T(128)}, u32[]{:S(2)}) copy-start(s32[128]{0:T(128)} %counts_hbm.1) | copy-start | bytes 1540
  0.7 40.8 %copy-start.6 = (f32[4,64,256]{2,1,0:T(8,128)S(1)}, f32[4,64,256]{2,1,0:T(8,128)}, u32[]{:S(2)}) copy-start(f32[4,64,256]{2,1,0:T(8,128)} %x_hbm.1) | copy-start | bytes 786436
